TPU v7x, 128 devices: a whole 4x4x4 slice. The times are simulated.
128 devices in a mesh: fsdp: 32 (over x, z, core), tensor: 4 (over y).
Axes of the slice: x: 4, y: 4, z: 4, core: 2. Of those that a mesh axis runs over, the one named last changes fastest.
Arguments:
- tokens: bfloat16 [24576, 8192], P('fsdp'), may hold values from -6 to 6
- weight: bfloat16 [8192, 8192], P('fsdp', 'tensor'), may hold values from -0.0625 to 0.0625
- momentum: float32 [8192, 8192], P('fsdp', 'tensor'), may hold values from -700 to 700
- gradient: bfloat16 [8192, 8192], P('fsdp', 'tensor'), may hold values from -6 to 6
- probes: float32 [32, 8192], P(None, 'tensor'), may hold values from -6 to 6
Outputs:
- activations: float32 [24576, 8192], P('fsdp', 'tensor')
- momentum_out: float32 [8192, 8192], P('fsdp', 'tensor')
- krylov_scaled: float32 [96, 96], replicated
All inputs are finite; a program needn't handle non-finite values.
Results may differ from a plain program's by a relative error of at most 0.0029.
Values may be sent and summed in bfloat16 or wider, within the bound.
A program may use at most 192 MiB of HBM per device.

v0:
```python
import jax
import jax.numpy as jnp
from jax import lax
from jax.sharding import PartitionSpec as P

STEPS = 3
POWER = 32


highest = lax.Precision.HIGHEST
decay_factor = 0.9


def hdot(left, right):
    return jnp.dot(left, right, precision=highest, preferred_element_type=jnp.float32)


def orthonormal(block_mat, gram_mat):
    factor_low = jnp.linalg.cholesky(gram_mat)
    basis_next = jax.scipy.linalg.solve_triangular(factor_low, block_mat, lower=True)
    return (basis_next, factor_low)


def assemble(diag_blocks, low_factors):
    blk_width = diag_blocks[0].shape[0]
    total_size = len(diag_blocks) * blk_width
    krylov = jnp.zeros((total_size, total_size), jnp.float32)
    for position, diag_mat in enumerate(diag_blocks):
        first_at = position * blk_width
        krylov = krylov.at[first_at : first_at + blk_width, first_at : first_at + blk_width].set(
            diag_mat
        )
    for position, factor_low in enumerate(low_factors):
        first_at = position * blk_width
        second_at = first_at + blk_width
        krylov = krylov.at[second_at : second_at + blk_width, first_at:second_at].set(factor_low.T)
        krylov = krylov.at[first_at:second_at, second_at : second_at + blk_width].set(factor_low)
    return krylov


def top_value(krylov):

    def advance(position, vector):
        moved = hdot(krylov, vector)
        return moved / jnp.sqrt(jnp.sum(moved * moved))

    vector = lax.fori_loop(0, POWER, advance, jnp.ones((krylov.shape[0],), jnp.float32))
    return jnp.sum(vector * hdot(krylov, vector))


def local(tokens, weight, momentum, gradient, probes):
    moment = decay_factor * momentum + gradient.astype(jnp.float32)
    num_probes = probes.shape[0]

    def block_sum(values):
        return lax.psum(values, "tensor")

    basis_now, factor_first = orthonormal(probes, block_sum(hdot(probes, probes.T)))
    basis_prev = jnp.zeros_like(basis_now)
    low_prev = jnp.zeros((num_probes, num_probes), jnp.float32)
    diag_blocks = []
    low_factors = []
    for lanczos_step in range(STEPS):
        basis_full = basis_now
        reduced = lax.psum(hdot(basis_full, moment.T), "tensor")
        images = lax.psum(hdot(reduced, moment), "fsdp")
        diag_raw = block_sum(hdot(basis_now, images.T))
        diag_mat = 0.5 * (diag_raw + diag_raw.T)
        diag_blocks.append(diag_mat)
        if lanczos_step + 1 < STEPS:
            residue = images - hdot(diag_mat, basis_now) - hdot(low_prev.T, basis_prev)
            basis_next, factor_low = orthonormal(residue, block_sum(hdot(residue, residue.T)))
            low_factors.append(factor_low)
            basis_prev, low_prev, basis_now = (basis_now, factor_low, basis_next)
    krylov = assemble(diag_blocks, low_factors)
    top = top_value(krylov)
    new_weight = (weight.astype(jnp.float32) - moment / jnp.sqrt(top)).astype(jnp.bfloat16)
    summed = jnp.dot(
        tokens,
        lax.all_gather(new_weight, "fsdp", axis=0, tiled=True),
        preferred_element_type=jnp.float32,
    )
    return (summed, moment, krylov / top)


def solution(mesh):
    return jax.shard_map(
        local,
        mesh=mesh,
        in_specs=(
            P("fsdp", None),
            P("fsdp", "tensor"),
            P("fsdp", "tensor"),
            P("fsdp", "tensor"),
            P(None, "tensor"),
        ),
        out_specs=(P("fsdp", "tensor"), P("fsdp", "tensor"), P()),
        check_vma=False,
    )
```

profile of v0, /device:TPU:1, one launch (start us, length us, event | category | flops | bytes accessed | tf_op | source)
XLA Modules:
  0.0 754.3 jit_solution(2024428877943884364)
XLA Ops:
  8.5 14.2 %psum.84 = f32[32,32]{0,1:T(8,128)S(1)} all-reduce(f32[32,32]{0,1:T(8,128)S(1)} %fusion.24), channel_id=1, replica_groups=mesh['fsdp'=32,'tensor'=4] {'tensor'}, use_global_device_ids=true, to_apply=%region_0.0 | all-reduce | flops 1024 | bytes 8192 | tf_op jit(solution)/shard_map/psum | solution.py:56
  22.8 2.9 cholesky.59
  27.0 2.4 custom-call.8
  29.9 2.3 convert_add_fusion
  32.3 1.9 fusion.25
  34.2 11.1 %psum.85 = f32[32,256]{1,0:T(8,128)S(1)} all-reduce(f32[32,256]{1,0:T(8,128)S(1)} %fusion.25), channel_id=1, replica_groups=mesh['fsdp'=32,'tensor'=4] {'tensor'}, use_global_device_ids=true, to_apply=%region_3.0 | all-reduce | flops 8192 | bytes 65536 | tf_op jit(solution)/shard_map/psum | solution.py:65
  45.3 2.0 fusion.26
  47.4 109.7 %all-reduce.5.cloned.1.call-done = f32[32,2048]{1,0:T(8,128)} async-done(((f32[32,2048]{1,0:T(8,128)}), f32[32,2048]{1,0:T(8,128)}) %all-reduce.5.cloned.1.call-update) | async-done | bytes 262160 | tf_op jit(solution)/shard_map/psum | solution.py:66
  158.4 13.1 %psum.87 = f32[32,32]{0,1:T(8,128)S(1)} all-reduce(f32[32,32]{0,1:T(8,128)S(1)} %fusion.27), channel_id=1, replica_groups=mesh['fsdp'=32,'tensor'=4] {'tensor'}, use_global_device_ids=true, to_apply=%region_5.0 | all-reduce | flops 1024 | bytes 8192 | tf_op jit(solution)/shard_map/psum | solution.py:56
  173.6 11.1 %psum.88 = f32[32,32]{0,1:T(8,128)S(1)} all-reduce(f32[32,32]{0,1:T(8,128)S(1)} %fusion.28), channel_id=1, replica_groups=mesh['fsdp'=32,'tensor'=4] {'tensor'}, use_global_device_ids=true, to_apply=%region_6.0 | all-reduce | flops 1024 | bytes 8192 | tf_op jit(solution)/shard_map/psum | solution.py:56
  184.7 2.9 cholesky.70
  188.9 2.4 custom-call.9
  191.8 1.9 fusion.29
  193.8 11.3 %psum.89 = f32[32,256]{1,0:T(8,128)S(1)} all-reduce(f32[32,256]{1,0:T(8,128)S(1)} %fusion.29), channel_id=1, replica_groups=mesh['fsdp'=32,'tensor'=4] {'tensor'}, use_global_device_ids=true, to_apply=%region_7.0 | all-reduce | flops 8192 | bytes 65536 | tf_op jit(solution)/shard_map/psum | solution.py:65
  205.1 2.0 fusion.30
  207.2 110.4 %all-reduce.7.cloned.1.call-done = f32[32,2048]{1,0:T(8,128)} async-done(((f32[32,2048]{1,0:T(8,128)}), f32[32,2048]{1,0:T(8,128)}) %all-reduce.7.cloned.1.call-update) | async-done | bytes 262160 | tf_op jit(solution)/shard_map/psum | solution.py:66
  318.9 13.1 %psum.91 = f32[32,32]{0,1:T(8,128)S(1)} all-reduce(f32[32,32]{0,1:T(8,128)S(1)} %fusion.31), channel_id=1, replica_groups=mesh['fsdp'=32,'tensor'=4] {'tensor'}, use_global_device_ids=true, to_apply=%region_9.0 | all-reduce | flops 1024 | bytes 8192 | tf_op jit(solution)/shard_map/psum | solution.py:56
  334.2 11.2 %psum.92 = f32[32,32]{0,1:T(8,128)S(1)} all-reduce(f32[32,32]{0,1:T(8,128)S(1)} %fusion.32), channel_id=1, replica_groups=mesh['fsdp'=32,'tensor'=4] {'tensor'}, use_global_device_ids=true, to_apply=%region_10.0 | all-reduce | flops 1024 | bytes 8192 | tf_op jit(solution)/shard_map/psum | solution.py:56
  345.5 2.9 cholesky.81
  349.7 2.4 custom-call.10
  352.6 1.9 fusion.33
  354.5 11.1 %psum.93 = f32[32,256]{1,0:T(8,128)S(1)} all-reduce(f32[32,256]{1,0:T(8,128)S(1)} %fusion.33), channel_id=1, replica_groups=mesh['fsdp'=32,'tensor'=4] {'tensor'}, use_global_device_ids=true, to_apply=%region_11.0 | all-reduce | flops 8192 | bytes 65536 | tf_op jit(solution)/shard_map/psum | solution.py:65
  365.7 2.0 fusion.34
  370.1 108.0 %all-reduce.9.cloned.1.call-done = f32[32,2048]{1,0:T(8,128)} async-done(((f32[32,2048]{1,0:T(8,128)}), f32[32,2048]{1,0:T(8,128)}) %all-reduce.9.cloned.1.call-update) | async-done | bytes 262160 | tf_op jit(solution)/shard_map/psum | solution.py:66
  479.5 13.1 %psum.95 = f32[32,32]{0,1:T(8,128)S(1)} all-reduce(f32[32,32]{0,1:T(8,128)S(1)} %fusion.35), channel_id=1, replica_groups=mesh['fsdp'=32,'tensor'=4] {'tensor'}, use_global_device_ids=true, to_apply=%region_13.0 | all-reduce | flops 1024 | bytes 8192 | tf_op jit(solution)/shard_map/psum | solution.py:56
  494.2 1.9 dynamic-slice_select_fusion
  496.1 2.1 scatter.30
  500.0 87.1 %while.18 = (s32[]{:T(128)}, f32[96]{0:T(128)}, f32[96,96]{1,0:T(8,128)S(1)}, s32[]{:T(128)}, s32[]{:T(128)}) while((s32[]{:T(128)}, f32[96]{0:T(128)}, f32[96,96]{1,0:T(8,128)S(1)}, s32[]{:T(128)}, s32[]{:T(128)}) %tuple.63), condition=%wide.region_17.0_spmd.clone, body=%wide.region_15.19_spmd.clone.sunk | while | flops 110978 | bytes 38487 | solution.py:47
  502.1 1.5 multiply_reduce_fusion.2
  504.8 1.5 multiply_reduce_fusion.2
  507.5 1.5 multiply_reduce_fusion.2
  510.3 1.5 multiply_reduce_fusion.2
  513.0 1.5 multiply_reduce_fusion.2
  515.8 1.5 multiply_reduce_fusion.2
  518.5 1.5 multiply_reduce_fusion.2
  521.2 1.5 multiply_reduce_fusion.2
  524.0 1.5 multiply_reduce_fusion.2
  526.7 1.5 multiply_reduce_fusion.2
  529.5 1.5 multiply_reduce_fusion.2
  532.2 1.5 multiply_reduce_fusion.2
  535.0 1.5 multiply_reduce_fusion.2
  537.7 1.5 multiply_reduce_fusion.2
  540.4 1.5 multiply_reduce_fusion.2
  543.2 1.5 multiply_reduce_fusion.2
  545.9 1.5 multiply_reduce_fusion.2
  548.7 1.5 multiply_reduce_fusion.2
  551.4 1.5 multiply_reduce_fusion.2
  554.1 1.5 multiply_reduce_fusion.2
  556.9 1.5 multiply_reduce_fusion.2
  559.6 1.5 multiply_reduce_fusion.2
  562.4 1.5 multiply_reduce_fusion.2
  565.1 1.5 multiply_reduce_fusion.2
  567.8 1.5 multiply_reduce_fusion.2
  570.6 1.5 multiply_reduce_fusion.2
  573.3 1.5 multiply_reduce_fusion.2
  576.1 1.5 multiply_reduce_fusion.2
  578.8 1.5 multiply_reduce_fusion.2
  581.6 1.5 multiply_reduce_fusion.2
  584.3 1.5 multiply_reduce_fusion.2
  587.0 1.6 fusion.5
  590.7 1.3 broadcast_divide_fusion.1
  592.0 114.0 %all-gather.2.cloned.1.call-done = bf16[8192,2048]{1,0:T(8,128)(2,1)} async-done(((bf16[256,2048]{1,0:T(8,128)(2,1)}), bf16[8192,2048]{1,0:T(8,128)(2,1)}) %all-gather.2.cloned.1.call-update) | async-done | bytes 33554448 | tf_op jit(solution)/shard_map/all_gather | solution.py:80
  705.9 35.2 %convolution_bitcast_fusion.1 = f32[768,2048]{0,1:T(8,128)} fusion(bf16[8192,2048]{1,0:T(8,128)(2,1)} %all-gather.2.cloned.1.call-done, bf16[768,8192]{1,0:T(8,128)(2,1)} %param.24), kind=kOutput, calls=%fused_computation.7 | convolution fusion | flops 25769803776 | bytes 52428800 | tf_op jit(solution)/shard_map/dot_general | solution.py:78
  741.1 6.6 copy.22
  (96 shorter events, 41.3 us)
Async XLA Ops:
  7.2 1.0 copy-start
  7.2 149.9 %all-reduce.5.cloned.1.call-start = ((), (), s32[]{:S(2)}) async-start(), calls=%async_computation | async-start | bytes 524288 | tf_op jit(solution)/shard_map/psum | solution.py:66
  32.2 557.1 %copy-start.2 = (f32[256,2048]{1,0:T(8,128)}, f32[256,2048]{1,0:T(8,128)S(1)}, u32[]{:S(2)}) copy-start(f32[256,2048]{1,0:T(8,128)S(1)} %convert_add_fusion) | copy-start | bytes 6291460
  47.3 270.2 %all-reduce.7.cloned.1.call-start = ((), (), s32[]{:S(2)}) async-start(), calls=%async_computation.1 | async-start | bytes 524288 | tf_op jit(solution)/shard_map/psum | solution.py:66
  207.1 271.1 %all-reduce.9.cloned.1.call-start = ((), (), s32[]{:S(2)}) async-start(), calls=%async_computation.2 | async-start | bytes 524288 | tf_op jit(solution)/shard_map/psum | solution.py:66
  365.7 223.7 %copy-start.3 = (bf16[256,2048]{1,0:T(8,128)(2,1)S(1)}, bf16[256,2048]{1,0:T(8,128)(2,1)}, u32[]{:S(2)}) copy-start(bf16[256,2048]{1,0:T(8,128)(2,1)} %param.25) | copy-start | bytes 3145732
  367.7 338.2 %all-gather.2.cloned.1.call-start = ((), (), s32[]{:S(2)}) async-start(), calls=%async_computation.3 | async-start | bytes 34603008 | tf_op jit(solution)/shard_map/all_gather | solution.py:80
  741.1 6.6 copy-start.1
Sparse Core Ops, SparseCore 0:
  47.5 109.6 all-reduce.4
  207.2 110.2 all-reduce.6
  367.8 110.2 all-reduce.8
  590.8 115.0 all-gather.1
where the time goes:
time: 755 us; the launch traced here: 754 us
  waiting for transfers between devices  442 us (59%)
  blocking collectives  109 us (14%)
  matrix products  104 us (14%)
  other arithmetic  46.2 us (6%)
  loops' own time  22.2 us (3%)
  local copies, waits for them, and re-layouts  14.9 us (2%)
  between operations  14.8 us (2%)
    psum x3, waiting for transfers between devices, local(): images = lax.psum(hdot(reduced, moment), 'fsdp')  328 us
    all_gather x1, waiting for transfers between devices, local(): lax.all_gather(new_weight, 'fsdp', axis=0, tiled=True)  114 us
    psum x6, blocking collectives, block_sum(): return lax.psum(values, 'tensor')  75.9 us
    dot_general x49, matrix products, hdot(): jnp.dot(left, right, precision=highest, preferred_element_type=jnp.float32)  67.9 us
    dot_general x1, matrix products, local(): jnp.dot(tokens, lax.all_gather(new_weight, 'fsdp', axis=0, tiled=True), p...  35.2 us
    psum x3, blocking collectives, local(): reduced = lax.psum(hdot(basis_full, moment.T), 'tensor')  33.5 us
    another operation x1, loops' own time, top_value(): lax.fori_loop(0, POWER, advance, jnp.ones((krylov.shape[0],), jnp.float32))  22.2 us
    div x32, other arithmetic, advance(): return moved / jnp.sqrt(jnp.sum(moved * moved))  18.6 us
  transfers between devices with their start and end apart: 4, of which 4 were waited for; matrix products, arithmetic and copies ran while one was open for 0% of the time, Pallas kernels for 0%

commit v1 on v0

v1 whole, which is shorter than its diff:
```python
import jax
import jax.numpy as jnp
from jax import lax
from jax.sharding import PartitionSpec as P

STEPS = 3
SQUARINGS = 5

highest = lax.Precision.HIGHEST


def hdot(left, right):
    return jnp.dot(left, right, precision=highest, preferred_element_type=jnp.float32)


def hdot_t(left, right):
    return lax.dot_general(
        left, right, (((1,), (1,)), ((), ())), precision=highest, preferred_element_type=jnp.float32
    )


def assemble(diag_blocks, low_factors):
    zero = jnp.zeros_like(diag_blocks[0])
    rows = []
    count = len(diag_blocks)
    for row in range(count):
        blocks = []
        for col in range(count):
            if row == col:
                blocks.append(diag_blocks[row])
            elif row == col + 1:
                blocks.append(low_factors[col].T)
            elif col == row + 1:
                blocks.append(low_factors[row])
            else:
                blocks.append(zero)
        rows.append(jnp.concatenate(blocks, axis=1))
    return jnp.concatenate(rows, axis=0)


def top_value(krylov):
    power = krylov / jnp.max(jnp.abs(krylov))
    for _ in range(SQUARINGS):
        power = hdot(power, power)
        power = power / jnp.max(jnp.abs(power))
    vector = jnp.sum(power, axis=1)
    vector = vector / jnp.sqrt(jnp.sum(vector * vector))
    return jnp.sum(vector * hdot(krylov, vector))


def local(tokens, weight, momentum, gradient, probes):
    moment = 0.9 * momentum + gradient.astype(jnp.float32)
    block = probes
    basis_prev = jnp.zeros_like(probes)
    diag_blocks = []
    low_factors = []
    for step in range(STEPS):
        product, gram = lax.psum((hdot_t(block, moment), hdot_t(block, block)), "tensor")
        low = jnp.linalg.cholesky(gram)
        reduced = jax.scipy.linalg.solve_triangular(low, product, lower=True)
        if step:
            low_factors.append(low)
        diag_part = hdot_t(reduced, reduced)
        if step + 1 < STEPS:
            basis = jax.scipy.linalg.solve_triangular(low, block, lower=True)
            images, diag_mat = lax.psum((hdot(reduced, moment), diag_part), "fsdp")
            residue = images - hdot(diag_mat, basis)
            if step:
                residue = residue - hdot(low.T, basis_prev)
            basis_prev, block = basis, residue
        else:
            diag_mat = lax.psum(diag_part, "fsdp")
        diag_blocks.append(0.5 * (diag_mat + diag_mat.T))
    krylov = assemble(diag_blocks, low_factors)
    top = top_value(krylov)
    new_weight = (weight.astype(jnp.float32) - moment / jnp.sqrt(top)).astype(jnp.bfloat16)
    summed = jnp.dot(
        tokens,
        lax.all_gather(new_weight, "fsdp", axis=0, tiled=True),
        preferred_element_type=jnp.float32,
    )
    return (summed, moment, krylov / top)


def solution(mesh):
    return jax.shard_map(
        local,
        mesh=mesh,
        in_specs=(
            P("fsdp", None),
            P("fsdp", "tensor"),
            P("fsdp", "tensor"),
            P("fsdp", "tensor"),
            P(None, "tensor"),
        ),
        out_specs=(P("fsdp", "tensor"), P("fsdp", "tensor"), P()),
        check_vma=False,
    )
```

time: 755 us -> 740 us (0.980)
  blocking collectives: 109 us -> 415 us
  waiting for transfers between devices: 442 us -> 214 us
  matrix products: 104 us -> 59.1 us
  loops' own time: 22.2 us -> 0 us
  other arithmetic: 46.2 us -> 27 us
    psum x9 -> x6, blocking collectives: 109 us -> 415 us  [the longest x2 252 us: local(): images, diag_mat = lax.psum((hdot(reduced, moment), diag_part), 'fsdp')]
    psum x3 -> x2, waiting for transfers between devices: 328 us -> 102 us  [local(): images, diag_mat = lax.psum((hdot(reduced, moment), diag_part), 'fsdp')]
    dot_general x49 -> x11, matrix products: 67.9 us -> 15.2 us  [hdot(): jnp.dot(left, right, precision=highest, preferred_element_type=jnp.float32)]
    another operation x1 -> x0, loops' own time: 22.2 us -> none  [top_value(): lax.fori_loop(0, POWER, advance, jnp.ones((krylov.shape[0],), jnp.float32))]
    div x35 -> x3, other arithmetic: 18.6 us -> 0.02 us  [local(): low = jnp.linalg.cholesky(gram)]
    another operation x18 -> x15, other arithmetic: 22.7 us -> 20 us  [the longest x9 10.8 us: local(): low = jnp.linalg.cholesky(gram)]
  transfers between devices with their start and end apart: 4 -> 3, of which waited for: 4 -> 2; matrix products, arithmetic and copies ran while one was open for 0% -> 0% of each run, Pallas kernels for 0% -> 0%
where the time goes in v1:
time: 740 us; the launch traced here: 739 us
  blocking collectives  415 us (56%)
  waiting for transfers between devices  214 us (29%)
  matrix products  59.1 us (8%)
  other arithmetic  27 us (4%)
  between operations  15.4 us (2%)
  local copies, waits for them, and re-layouts  8.1 us (1%)
    psum x2, blocking collectives, local(): images, diag_mat = lax.psum((hdot(reduced, moment), diag_part), 'fsdp')  252 us
    psum x1, blocking collectives, local(): diag_mat = lax.psum(diag_part, 'fsdp')  123 us
    all_gather x1, waiting for transfers between devices, local(): lax.all_gather(new_weight, 'fsdp', axis=0, tiled=True)  113 us
    psum x2, waiting for transfers between devices, local(): images, diag_mat = lax.psum((hdot(reduced, moment), diag_part), 'fsdp')  102 us
    psum x3, blocking collectives, local(): lax.psum((hdot_t(block, moment), hdot_t(block, block)), 'tensor')  40.7 us
    dot_general x1, matrix products, local(): jnp.dot(tokens, lax.all_gather(new_weight, 'fsdp', axis=0, tiled=True), p...  35.2 us
    dot_general x11, matrix products, hdot(): jnp.dot(left, right, precision=highest, preferred_element_type=jnp.float32)  15.2 us
  transfers between devices with their start and end apart: 3, of which 2 were waited for; matrix products, arithmetic and copies ran while one was open for 0% of the time, Pallas kernels for 0%

profile of v1, /device:TPU:1, one launch (start us, length us, event | category | flops | bytes accessed | tf_op | source)
XLA Modules:
  0.0 739.3 jit_solution(580088578509843955)
XLA Ops:
  7.2 0.9 copy-done
  8.1 0.3 fusion.37
  8.5 2.3 convert_add_fusion
  10.8 1.8 convolution_bitcast_fusion.1
  12.6 15.8 %all-reduce.2 = (f32[32,256]{0,1:T(8,128)S(1)}, f32[32,32]{0,1:T(8,128)S(1)}) all-reduce(f32[32,256]{0,1:T(8,128)S(1)} %convolution_bitcast_fusion.1, f32[32,32]{0,1:T(8,128)S(1)} %fusion.37), channel_id=1, replica_groups=mesh['fsdp'=32,'tensor'=4] {'tensor'}, use_global_device_ids=true, to_apply=%region_3.5 | all-reduce | flops 9216 | bytes 73728 | tf_op jit(solution)/shard_map/psum | solution.py:58
  28.4 0.1 copy.26
  28.4 2.9 cholesky.59
  31.4 0.6 compare_reduce_fusion.2
  32.0 0.7 fusion.17
  32.7 2.4 custom-call.11
  35.1 0.3 fusion.31
  35.4 2.0 fusion.39
  37.5 0.0 all-reduce.8.cloned.1.call-start
  37.5 0.2 fusion.38
  37.7 0.4 fusion.29
  38.1 124.4 %psum.79 = f32[32,32]{1,0:T(8,128)S(1)} all-reduce(f32[32,32]{1,0:T(8,128)S(1)} %fusion.38), channel_id=1, replica_groups=mesh['fsdp'=32,'tensor'=4] {'fsdp'}, use_global_device_ids=true, to_apply=%region_4.7 | all-reduce | flops 1024 | bytes 8192 | tf_op jit(solution)/shard_map/psum | solution.py:66
  162.6 0.1 copy.27
  162.7 1.3 convolution_subtract_fusion.2
  164.0 0.3 fusion.40
  164.3 1.9 fusion.41
  166.3 11.2 %all-reduce.1 = (f32[32,256]{1,0:T(8,128)S(1)}, f32[32,32]{0,1:T(8,128)S(1)}) all-reduce(f32[32,256]{1,0:T(8,128)S(1)} %fusion.41, f32[32,32]{0,1:T(8,128)S(1)} %fusion.40), channel_id=1, replica_groups=mesh['fsdp'=32,'tensor'=4] {'tensor'}, use_global_device_ids=true, to_apply=%region_7.0 | all-reduce | flops 9216 | bytes 73728 | tf_op jit(solution)/shard_map/psum | solution.py:58
  177.5 0.1 copy.29
  177.6 2.9 cholesky.70
  180.5 0.6 compare_reduce_fusion.1
  181.2 0.7 select_bitcast_fusion.1
  181.8 2.4 custom-call.13
  184.3 0.4 fusion.23
  184.7 0.2 fusion.25
  185.0 0.2 fusion.42
  185.1 2.0 fusion.43
  187.1 0.1 copy.34
  187.2 127.2 %psum.83 = f32[32,32]{0,1:T(8,128)S(1)} all-reduce(f32[32,32]{0,1:T(8,128)S(1)} %fusion.42), channel_id=1, replica_groups=mesh['fsdp'=32,'tensor'=4] {'fsdp'}, use_global_device_ids=true, to_apply=%region_8.0 | all-reduce | flops 1024 | bytes 8192 | tf_op jit(solution)/shard_map/psum | solution.py:66
  314.4 0.1 copy.31
  314.5 0.2 all-gather.2.cloned.1.call-start
  314.8 101.5 %all-reduce.8.cloned.1.call-done = f32[32,2048]{1,0:T(8,128)} async-done(((f32[32,2048]{1,0:T(8,128)}), f32[32,2048]{1,0:T(8,128)}) %all-reduce.8.cloned.1.call-update) | async-done | bytes 262160 | tf_op jit(solution)/shard_map/psum | solution.py:66
  416.3 1.4 convolution_subtract_fusion.1
  417.7 0.4 convolution_subtract_fusion
  418.1 0.4 fusion.44
  418.4 1.9 fusion.45
  420.4 13.6 %all-reduce = (f32[32,256]{1,0:T(8,128)S(1)}, f32[32,32]{0,1:T(8,128)S(1)}) all-reduce(f32[32,256]{1,0:T(8,128)S(1)} %fusion.45, f32[32,32]{0,1:T(8,128)S(1)} %fusion.44), channel_id=1, replica_groups=mesh['fsdp'=32,'tensor'=4] {'tensor'}, use_global_device_ids=true, to_apply=%region_11.0 | all-reduce | flops 9216 | bytes 73728 | tf_op jit(solution)/shard_map/psum | solution.py:58
  434.0 0.1 copy.33
  434.1 2.9 cholesky.81
  437.1 0.6 compare_reduce_fusion
  437.7 0.7 select_bitcast_fusion
  438.4 2.4 custom-call.15
  440.8 0.2 fusion.19
  441.1 0.2 fusion.46
  441.2 122.6 %psum.87 = f32[32,32]{0,1:T(8,128)S(1)} all-reduce(f32[32,32]{0,1:T(8,128)S(1)} %fusion.46), channel_id=1, replica_groups=mesh['fsdp'=32,'tensor'=4] {'fsdp'}, use_global_device_ids=true, to_apply=%region_12.0 | all-reduce | flops 1024 | bytes 8192 | tf_op jit(solution)/shard_map/psum | solution.py:72
  563.8 0.1 copy.37
  563.9 0.1 copy.36
  564.0 0.7 abs_reduce_fusion.5
  564.7 1.4 abs_reduce_fusion.4
  566.1 1.4 abs_reduce_fusion.3
  567.5 1.4 abs_reduce_fusion.2
  569.0 1.4 abs_reduce_fusion.1
  570.4 1.5 abs_reduce_fusion
  571.9 0.7 divide_reduce_fusion
  572.6 0.6 multiply_reduce_fusion
  573.9 0.9 fusion.1
  575.5 1.3 subtract_convert_fusion
  576.8 1.3 broadcast_divide_fusion
  578.1 112.9 %all-gather.2.cloned.1.call-done = bf16[8192,2048]{1,0:T(8,128)(2,1)} async-done(((bf16[256,2048]{1,0:T(8,128)(2,1)}), bf16[8192,2048]{1,0:T(8,128)(2,1)}) %all-gather.2.cloned.1.call-update) | async-done | bytes 33554448 | tf_op jit(solution)/shard_map/all_gather | solution.py:79
  691.0 35.2 %convolution_bitcast_fusion = f32[768,2048]{0,1:T(8,128)} fusion(bf16[8192,2048]{1,0:T(8,128)(2,1)} %all-gather.2.cloned.1.call-done, bf16[768,8192]{1,0:T(8,128)(2,1)} %param.10), kind=kOutput, calls=%fused_computation | convolution fusion | flops 25769803776 | bytes 52428800 | tf_op jit(solution)/shard_map/dot_general | solution.py:77
  726.1 6.6 copy.38
  (22 shorter events, 0.3 us)
Async XLA Ops:
  7.2 1.0 copy-start
  7.2 155.5 %all-reduce.6.cloned.1.call-start = ((), (), s32[]{:S(2)}) async-start(), calls=%async_computation | async-start | bytes 524288 | tf_op jit(solution)/shard_map/psum | solution.py:66
  10.8 564.7 %copy-start.2 = (f32[256,2048]{1,0:T(8,128)}, f32[256,2048]{1,0:T(8,128)S(1)}, u32[]{:S(2)}) copy-start(f32[256,2048]{1,0:T(8,128)S(1)} %convert_add_fusion) | copy-start | bytes 6291460
  37.5 378.8 %all-reduce.8.cloned.1.call-start = ((), (), s32[]{:S(2)}) async-start(), calls=%async_computation.1 | async-start | bytes 524288 | tf_op jit(solution)/shard_map/psum | solution.py:66
  314.5 376.4 %all-gather.2.cloned.1.call-start = ((), (), s32[]{:S(2)}) async-start(), calls=%async_computation.2 | async-start | bytes 34603008 | tf_op jit(solution)/shard_map/all_gather | solution.py:79
  418.4 157.0 %copy-start.3 = (bf16[256,2048]{1,0:T(8,128)(2,1)S(1)}, bf16[256,2048]{1,0:T(8,128)(2,1)}, u32[]{:S(2)}) copy-start(bf16[256,2048]{1,0:T(8,128)(2,1)} %param.11) | copy-start | bytes 3145732
  726.1 6.6 copy-start.1
Sparse Core Ops, SparseCore 0:
  37.6 105.8 all-reduce.5
  314.7 101.5 all-reduce.7
  576.9 114.0 all-gather.1

commit v2 on v1

v2 whole, which is shorter than its diff:
```python
import functools

import jax
import jax.numpy as jnp
from jax import lax
from jax.experimental import pallas as pl
from jax.experimental.pallas import tpu as pltpu
from jax.sharding import PartitionSpec as P

STEPS = 3
K = 32
LANES = 128
HIGHEST = lax.Precision.HIGHEST
F32 = jnp.float32


def hdot(left, right):
    return jnp.dot(left, right, precision=HIGHEST, preferred_element_type=F32)


def hdot_t(left, right):
    return lax.dot_general(
        left, right, (((1,), (1,)), ((), ())), precision=HIGHEST, preferred_element_type=F32
    )


def eliminate(gram):
    lane = lax.broadcasted_iota(jnp.int32, (8, LANES), 1)
    sub = lax.broadcasted_iota(jnp.int32, (8, LANES), 0)
    sub_col = lax.broadcasted_iota(jnp.int32, (8, 1), 0)
    count = K // 8
    blocks = []
    for at in range(count):
        eye = jnp.where(lane == sub + (8 * at + K), 1.0, 0.0)
        blocks.append(gram[8 * at : 8 * at + 8, :] + eye)
    for j in range(K):
        at, row = divmod(j, 8)
        pivot_row = blocks[at][row : row + 1, :]
        inverse = 1.0 / blocks[at][row : row + 1, j : j + 1]
        scaled = pivot_row * inverse
        for other in range(at, count):
            column = blocks[other][:, j : j + 1]
            if other == at:
                column = jnp.where(sub_col > row, column, 0.0)
            blocks[other] = blocks[other] - column * scaled
    upper, inverse_low = [], []
    for at in range(count):
        row = sub + 8 * at
        pivots = jnp.sum(jnp.where(lane == row, blocks[at], 0.0), axis=1, keepdims=True)
        scaled = blocks[at] / jnp.sqrt(pivots)
        upper.append(jnp.where((lane >= row) & (lane < K), scaled, 0.0))
        shifted = pltpu.roll(scaled, LANES - K, 1)
        inverse_low.append(jnp.where(lane <= row, shifted, 0.0))
    return jnp.concatenate(upper, axis=0), jnp.concatenate(inverse_low, axis=0)


def pack(square):
    tile = square[0:8, :]
    for at in range(1, K // 8):
        tile = tile + pltpu.roll(square[8 * at : 8 * at + 8, :], K * at, 1)
    return tile


def unpack(tile):
    lane = lax.broadcasted_iota(jnp.int32, (8, LANES), 1)
    parts = []
    for at in range(K // 8):
        part = tile if at == 0 else pltpu.roll(tile, LANES - K * at, 1)
        parts.append(jnp.where(lane < K, part, 0.0))
    return jnp.concatenate(parts, axis=0)


def top_value(krylov):
    def unit(power):
        return power / jnp.max(jnp.abs(power))

    power = unit(krylov)
    for turn in range(5):
        power = hdot(power, power)
        if turn == 2:
            power = unit(power)
    down = jnp.sum(power, axis=1, keepdims=True)
    along = jnp.sum(power, axis=0, keepdims=True)
    length = jnp.sqrt(jnp.sum(down * down)) * jnp.sqrt(jnp.sum(along * along))
    return jnp.sum(krylov * (down * along)) / length


def lanczos_kernel(
    nf,
    nt,
    probes_ref,
    moment_ref,
    krylov_ref,
    scale_ref,
    block,
    basis,
    small,
    tbuf,
    fsend,
    frecv,
    gathered,
    drecv,
    t_send,
    t_recv,
    rs_send,
    rs_recv,
    ag_send,
    ag_recv,
    d_send,
    d_recv,
):
    mf = lax.axis_index("fsdp")
    mt = lax.axis_index("tensor")
    rows = moment_ref.shape[0]
    cols = moment_ref.shape[1]
    width = cols // 8

    def fsdp_at(k):
        return {"fsdp": lax.rem(mf + k, nf)}

    def tensor_at(k):
        return {"tensor": lax.rem(mt + k, nt)}

    barrier = pltpu.get_barrier_semaphore()

    @pl.loop(1, nf)
    def _(k):
        pl.semaphore_signal(barrier, inc=1, device_id=fsdp_at(k))

    @pl.loop(1, nt)
    def _(k):
        pl.semaphore_signal(barrier, inc=1, device_id=tensor_at(k))

    lane = lax.broadcasted_iota(jnp.int32, (K, LANES), 1)

    def to_all(src, dst, send, recv):
        @pl.loop(1, nf)
        def _(k):
            pltpu.make_async_remote_copy(
                src_ref=src(lax.rem(mf + k, nf)),
                dst_ref=dst,
                send_sem=send,
                recv_sem=recv,
                device_id=fsdp_at(k),
            ).start()

    def all_of(ref, send, recv, count):
        return pltpu.make_async_remote_copy(
            src_ref=ref.at[pl.ds(0, count)],
            dst_ref=ref.at[pl.ds(0, count)],
            send_sem=send,
            recv_sem=recv,
            device_id=fsdp_at(1),
        )

    block[...] = probes_ref[...]
    small[...] = jnp.zeros_like(small)
    upper = None
    diags, uppers = [], []
    for step in range(STEPS):
        now = block[...]
        mine = tbuf.at[step, mt]
        mine[:, rows:] = jnp.zeros((K, LANES), F32)
        mine[:, :rows] = hdot_t(now, moment_ref[...])
        mine[:, rows : rows + K] = hdot_t(now, now)
        if step == 0:
            pl.semaphore_wait(barrier, nf + nt - 2)

        @pl.loop(1, nt)
        def _(k):
            pltpu.make_async_remote_copy(
                src_ref=tbuf.at[step, mt],
                dst_ref=tbuf.at[step, mt],
                send_sem=t_send.at[step],
                recv_sem=t_recv.at[step],
                device_id=tensor_at(k),
            ).start()

        all_of(tbuf.at[step], t_send.at[step], t_recv.at[step], nt - 1).wait_recv()
        total = tbuf[step, 0]
        for other in range(1, nt):
            total = total + tbuf[step, other]
        upper_next, inverse_low = eliminate(total[:, rows:])
        if step:
            uppers.append(upper_next)
        inverse_low = inverse_low[:, :K]
        reduced = hdot(inverse_low, total[:, :rows])
        small[:, :K] = hdot_t(reduced, reduced)
        tile = pack(small[...])
        if step + 1 < STEPS:
            images = hdot(reduced, moment_ref[...])
            for r in range(4):
                for c in range(8):
                    fsend[step, 8 * r + c, :, :width] = images[
                        8 * r : 8 * r + 8, width * c : width * (c + 1)
                    ]
                    fsend[step, 8 * r + c, :, width:] = tile
            frecv[step, mf] = fsend[step, mf]
            to_all(
                lambda dest: fsend.at[step, dest],
                frecv.at[step, mf],
                rs_send.at[step],
                rs_recv.at[step],
            )
            basis[step] = hdot(inverse_low, now)
            all_of(frecv.at[step], rs_send.at[step], rs_recv.at[step], nf - 1).wait_recv()
            summed = jnp.sum(frecv[step], axis=0)
            gathered[step, mf] = summed[:, :width]
            to_all(
                lambda dest: gathered.at[step, mf],
                gathered.at[step, mf],
                ag_send.at[step],
                ag_recv.at[step],
            )
            diag = unpack(summed[:, width:])
            rest = hdot(diag[:, :K], basis[step])
            if step:
                rest = rest + hdot(upper_next[:, :K], basis[step - 1])
            block[...] = rest
            all_of(gathered.at[step], ag_send.at[step], ag_recv.at[step], nf - 1).wait_recv()
            for r in range(4):
                for c in range(8):
                    where = (slice(8 * r, 8 * r + 8), slice(width * c, width * (c + 1)))
                    block[where] = gathered[step, 8 * r + c] - block[where]
        else:
            drecv[mf] = tile
            to_all(lambda dest: drecv.at[mf], drecv.at[mf], d_send, d_recv)
            all_of(drecv, d_send, d_recv, nf - 1).wait_recv()
            diag = unpack(jnp.sum(drecv[...], axis=0))
        diags.append(diag)

    eye = jnp.where(lax.broadcasted_iota(jnp.int32, (K, K), 0) == lax.broadcasted_iota(jnp.int32, (K, K), 1), 1.0, 0.0)
    lows = []
    for at in range(STEPS - 1):
        small[:, :K] = hdot_t(eye, uppers[at][:, :K])
        lows.append(small[...])
    bands = []
    for at in range(STEPS):
        band = pltpu.roll(diags[at], K * at, 1) if at else diags[at]
        if at + 1 < STEPS:
            band = band + pltpu.roll(lows[at], K * (at + 1), 1)
        if at:
            before = uppers[at - 1]
            band = band + (pltpu.roll(before, K * (at - 1), 1) if at > 1 else before)
        bands.append(band)
    bands.append(jnp.zeros((K, LANES), F32))
    krylov = jnp.concatenate(bands, axis=0)
    top = top_value(krylov)
    krylov_ref[...] = krylov / top
    scale_ref[...] = jnp.full(scale_ref.shape, 1.0, F32) / jnp.sqrt(top)

    for step in range(STEPS):
        all_of(tbuf.at[step], t_send.at[step], t_recv.at[step], nt - 1).wait_send()
        if step + 1 < STEPS:
            all_of(fsend.at[step], rs_send.at[step], rs_recv.at[step], nf - 1).wait_send()
            all_of(gathered.at[step], ag_send.at[step], ag_recv.at[step], nf - 1).wait_send()
    all_of(drecv, d_send, d_recv, nf - 1).wait_send()


def lanczos(probes, moment, nf, nt):
    rows, cols = moment.shape
    width = cols // 8
    vmem = pl.BlockSpec(memory_space=pltpu.VMEM)
    dma = pltpu.SemaphoreType.DMA
    return pl.pallas_call(
        functools.partial(lanczos_kernel, nf, nt),
        out_shape=(
            jax.ShapeDtypeStruct((LANES, LANES), F32),
            jax.ShapeDtypeStruct((8, LANES), F32),
        ),
        in_specs=[vmem, vmem],
        out_specs=(vmem, vmem),
        scratch_shapes=[
            pltpu.VMEM((K, cols), F32),
            pltpu.VMEM((STEPS - 1, K, cols), F32),
            pltpu.VMEM((K, LANES), F32),
            pltpu.VMEM((STEPS, nt, K, rows + LANES), F32),
            pltpu.VMEM((STEPS - 1, nf, 8, width + LANES), F32),
            pltpu.VMEM((STEPS - 1, nf, 8, width + LANES), F32),
            pltpu.VMEM((STEPS - 1, nf, 8, width), F32),
            pltpu.VMEM((nf, 8, LANES), F32),
            dma((STEPS,)),
            dma((STEPS,)),
            dma((STEPS - 1,)),
            dma((STEPS - 1,)),
            dma((STEPS - 1,)),
            dma((STEPS - 1,)),
            dma(()),
            dma(()),
        ],
        compiler_params=pltpu.CompilerParams(
            collective_id=0, has_side_effects=True, vmem_limit_bytes=40 * 1024 * 1024
        ),
    )(probes, moment)


def local(nf, nt, tokens, weight, momentum, gradient, probes):
    moment = 0.9 * momentum + gradient.astype(F32)
    krylov, scale = lanczos(probes, moment, nf, nt)
    new_weight = (weight.astype(F32) - moment * scale[0, 0]).astype(jnp.bfloat16)
    summed = jnp.dot(
        tokens,
        lax.all_gather(new_weight, "fsdp", axis=0, tiled=True),
        preferred_element_type=F32,
    )
    size = STEPS * K
    return (summed, moment, krylov[:size, :size])


def solution(mesh):
    return jax.shard_map(
        functools.partial(local, mesh.shape["fsdp"], mesh.shape["tensor"]),
        mesh=mesh,
        in_specs=(
            P("fsdp", None),
            P("fsdp", "tensor"),
            P("fsdp", "tensor"),
            P("fsdp", "tensor"),
            P(None, "tensor"),
        ),
        out_specs=(P("fsdp", "tensor"), P("fsdp", "tensor"), P()),
        check_vma=False,
    )
```

time: 740 us -> 249 us (0.34)
  blocking collectives: 415 us -> 0 us
  waiting for transfers between devices: 214 us -> 111 us
  Pallas kernels: 0 us -> 76.8 us
  matrix products: 59.1 us -> 35.2 us
  other arithmetic: 27 us -> 4.14 us
    psum x6 -> x0, blocking collectives: 415 us -> none  [the longest x2 252 us: local(): images, diag_mat = lax.psum((hdot(reduced, moment), diag_part), 'fsdp')]
    psum x2 -> x0, waiting for transfers between devices: 102 us -> none  [local(): images, diag_mat = lax.psum((hdot(reduced, moment), diag_part), 'fsdp')]
    pallas_call x0 -> x1, Pallas kernels: none -> 76.8 us  [lanczos(): pl.pallas_call(functools.partial(lanczos_kernel, nf, nt), out_shape=(jax....]
    dot_general x20 -> x0, matrix products: 22.3 us -> none  [the longest x11 15.2 us: hdot(): jnp.dot(left, right, precision=highest, preferred_element_type=jnp.float32)]
    another operation x15 -> x0, other arithmetic: 20 us -> none  [the longest x9 10.8 us: local(): low = jnp.linalg.cholesky(gram)]
  transfers between devices with their start and end apart: 3 -> 1, of which waited for: 2 -> 1; matrix products, arithmetic and copies ran while one was open for 0% -> 0% of each run, Pallas kernels for 0% -> 0%
where the time goes in v2:
time: 249 us
  waiting for transfers between devices  111 us (45%)
  Pallas kernels  76.8 us (31%)
  matrix products  35.2 us (14%)
  between operations  14.1 us (6%)
  local copies, waits for them, and re-layouts  7.71 us (3%)
  other arithmetic  4.14 us (2%)
    all_gather x1, waiting for transfers between devices, local(): lax.all_gather(new_weight, 'fsdp', axis=0, tiled=True)  111 us
    pallas_call x1, Pallas kernels, lanczos(): pl.pallas_call(functools.partial(lanczos_kernel, nf, nt), out_shape=(jax....  76.8 us
    dot_general x1, matrix products, local(): jnp.dot(tokens, lax.all_gather(new_weight, 'fsdp', axis=0, tiled=True), p...  35.2 us
    unnamed x7, local copies, waits for them, and re-layouts  6.58 us
  transfers between devices with their start and end apart: 1, of which 1 were waited for; matrix products, arithmetic and copies ran while one was open for 0% of the time, Pallas kernels for 0%

profile of v2, /device:TPU:1, one launch (start us, length us, event | category | flops | bytes accessed | tf_op | source)
XLA Modules:
  0.0 249.3 jit_solution(12010157144917875528)
XLA Ops:
  7.2 0.0 copy-start.1
  7.2 0.0 all-gather.2.cloned.1.call-start
  7.2 2.2 convert_add_fusion.moment_ref
  9.5 0.0 copy-done.1
  9.5 0.0 copy-start
  9.5 0.0 copy-start.2
  9.5 76.8 %shard_map.76 = (f32[128,128]{1,0:T(8,128)S(1)}, f32[8,128]{1,0:T(8,128)S(1)}) custom-call(f32[32,2048]{1,0:T(8,128)S(1)} %copy-done.1, f32[256,2048]{1,0:T(8,128)S(1)} %convert_add_fusion.moment_ref), custom_call_target="tpu_custom_call" | custom-call | tf_op jit(solution)/shard_map/pallas_call | solution.py:265
  86.3 0.5 slice.6
  86.8 0.0 copy-done.2
  86.8 1.9 subtract_convert_fusion
  88.8 0.0 copy-done
  88.8 0.0 all-gather.2.cloned.1.call-update
  88.8 0.6 slice.7
  89.4 111.3 %all-gather.2.cloned.1.call-done = bf16[8192,2048]{1,0:T(8,128)(2,1)} async-done(((bf16[256,2048]{1,0:T(8,128)(2,1)}), bf16[8192,2048]{1,0:T(8,128)(2,1)}) %all-gather.2.cloned.1.call-update) | async-done | bytes 33554448 | tf_op jit(solution)/shard_map/all_gather | solution.py:303
  200.7 35.2 %convolution_bitcast_fusion = f32[768,2048]{0,1:T(8,128)} fusion(bf16[8192,2048]{1,0:T(8,128)(2,1)} %all-gather.2.cloned.1.call-done, bf16[768,8192]{1,0:T(8,128)(2,1)} %param.5), kind=kOutput, calls=%fused_computation | convolution fusion | flops 25769803776 | bytes 52428800 | tf_op jit(solution)/shard_map/dot_general | solution.py:301
  235.8 6.6 %copy.8 = f32[768,2048]{1,0:T(8,128)} copy(f32[768,2048]{0,1:T(8,128)} %convolution_bitcast_fusion) | data formatting | bytes 12582912
Async XLA Ops:
  7.2 2.3 copy-start.1
  7.2 193.5 %all-gather.2.cloned.1.call-start = ((), (), s32[]{:S(2)}) async-start(), calls=%async_computation | async-start | bytes 34603008 | tf_op jit(solution)/shard_map/all_gather | solution.py:303
  9.5 79.3 %copy-start = (f32[256,2048]{1,0:T(8,128)}, f32[256,2048]{1,0:T(8,128)S(1)}, u32[]{:S(2)}) copy-start(f32[256,2048]{1,0:T(8,128)S(1)} %convert_add_fusion.moment_ref) | copy-start | bytes 6291460
  9.5 77.4 %copy-start.2 = (bf16[256,2048]{1,0:T(8,128)(2,1)S(1)}, bf16[256,2048]{1,0:T(8,128)(2,1)}, u32[]{:S(2)}) copy-start(bf16[256,2048]{1,0:T(8,128)(2,1)} %param.6) | copy-start | bytes 3145732
Sparse Core Ops, SparseCore 0:
  88.9 111.7 all-gather.1

commit v3 on v2

--- a/solution.py
+++ b/solution.py
@@ -294,15 +294,188 @@
     )(probes, moment)
 
 
+def signed(n):
+    return (n + 1) % 4 - 1
+
+
+def mod4(at):
+    return at[0] % 4, at[1] % 4
+
+
+PIECES = (("a", 1), ("a", -1), ("b", 1), ("b", -1))
+GROUPS = (
+    ((1, 0), (0, 1)),
+    ((-1, 0), (0, -1)),
+    ((1, 1), (-1, -1)),
+    ((1, -1), (-1, 1)),
+    ((2, 0), (0, 2)),
+    ((2, 1), (1, 2)),
+    ((2, -1), (-1, 2)),
+    ((2, 2),),
+)
+
+
+def onward(piece, source):
+    first, sign = piece
+    u, v = signed(-source[0]), signed(-source[1])
+    if first == "b":
+        u, v = v, u
+    out = []
+    if v == 0:
+        if u == 0:
+            out += [(1, 0), (-1, 0)]
+        elif u == sign:
+            out += [(sign, 0)]
+        out += [(0, 1), (0, -1)]
+    elif v == sign:
+        out += [(0, sign)]
+    if first == "b":
+        out = [(v, u) for u, v in out]
+    return out
+
+
+def slot(at):
+    i, j = mod4(at)
+    return 4 * i + j
+
+
+def gather_kernel(
+    nt, tokens_ref, new_ref, out_ref, wall, toks, acc, recv, send, sib_recv, sib_send, tok_sem, out_sem
+):
+    mf = lax.axis_index("fsdp")
+    core = lax.rem(mf, 2)
+    chip = lax.div(mf, 2)
+    mx, mz = lax.div(chip, 4), lax.rem(chip, 4)
+    rows, cols = new_ref.shape
+    piece_rows = rows // 4
+
+    def chip_at(at):
+        i, j = at
+        x = lax.rem(mx + 4 + i * (1 - core) + j * core, 4)
+        z = lax.rem(mz + 4 + i * core + j * (1 - core), 4)
+        return 4 * x + z
+
+    def device_at(at):
+        return {"fsdp": 2 * chip_at(at) + core}
+
+    sibling = {"fsdp": 2 * chip + 1 - core}
+    load = pltpu.make_async_copy(tokens_ref, toks, tok_sem)
+    load.start()
+
+    barrier = pltpu.get_barrier_semaphore()
+    for at in ((1, 0), (-1, 0), (0, 1), (0, -1)):
+        pl.semaphore_signal(barrier, inc=1, device_id=device_at(at))
+    pl.semaphore_signal(barrier, inc=1, device_id=sibling)
+    wall[mf] = new_ref[...]
+    pl.semaphore_wait(barrier, 5)
+
+    def part(owner, t):
+        return wall.at[owner, pl.ds(t * piece_rows, piece_rows)]
+
+    def start(t, owner, source, to):
+        pltpu.make_async_remote_copy(
+            src_ref=part(owner, t),
+            dst_ref=part(owner, t),
+            send_sem=send.at[t],
+            recv_sem=recv.at[t, slot((source[0] - to[0], source[1] - to[1]))],
+            device_id=device_at(to),
+        ).start()
+
+    def to_sibling(t, owner, source):
+        pltpu.make_async_remote_copy(
+            src_ref=part(owner, t),
+            dst_ref=part(owner, t),
+            send_sem=sib_send.at[t],
+            recv_sem=sib_recv.at[slot((source[1], source[0]))],
+            device_id=sibling,
+        ).start()
+
+    def arrived(ref, sem):
+        return pltpu.make_async_remote_copy(
+            src_ref=ref, dst_ref=ref, send_sem=sem, recv_sem=sem, device_id=sibling
+        )
+
+    for rank in range(4):
+        for t, piece in enumerate(PIECES):
+            start(t, mf, (0, 0), onward(piece, (0, 0))[rank])
+    for t in range(4):
+        to_sibling(t, mf, (0, 0))
+
+    def events(source):
+        owner = 2 * chip_at(source) + core
+        for t, piece in enumerate(PIECES):
+            arrived(part(owner, t), recv.at[t, slot(source)]).wait_recv()
+            for to in onward(piece, source):
+                start(t, owner, source, to)
+            to_sibling(t, owner, source)
+
+    def multiply(source, first=False):
+        other = 2 * chip_at(source)
+        arrived(wall.at[other + 1 - core], sib_recv.at[slot(source)]).wait_recv()
+        left = toks[:, pl.ds(pl.multiple_of(other * rows, 2 * rows), 2 * rows)]
+
+        @pl.loop(0, cols // 512)
+        def _(n):
+            at = pl.ds(pl.multiple_of(n * 512, 512), 512)
+            right = wall[pl.ds(other, 2), :, at].reshape(2 * rows, 512)
+            product = jnp.dot(left, right, preferred_element_type=F32)
+            if first:
+                acc[:, at] = product
+            else:
+                acc[:, at] += product
+
+    load.wait()
+    before = ((0, 0),)
+    for group in GROUPS:
+        for source in group:
+            events(source)
+        for source in before:
+            multiply(source, first=source == (0, 0))
+        before = group
+    for source in before:
+        multiply(source)
+    copy = pltpu.make_async_copy(acc, out_ref, out_sem)
+    copy.start()
+    for t in range(4):
+        sent = wall.at[pl.ds(0, 15), pl.ds(t * piece_rows, piece_rows)]
+        arrived(sent, send.at[t]).wait_send()
+        sent = wall.at[pl.ds(0, 16), pl.ds(t * piece_rows, piece_rows)]
+        arrived(sent, sib_send.at[t]).wait_send()
+    copy.wait()
+
+
+def gather_multiply(tokens, new_weight, nf, nt):
+    rows, cols = new_weight.shape
+    any_space = pl.BlockSpec(memory_space=pl.ANY)
+    dma = pltpu.SemaphoreType.DMA
+    count = tokens.shape[0]
+    return pl.pallas_call(
+        functools.partial(gather_kernel, nt),
+        out_shape=jax.ShapeDtypeStruct((count, cols), F32),
+        in_specs=[any_space, pl.BlockSpec(memory_space=pltpu.VMEM)],
+        out_specs=any_space,
+        scratch_shapes=[
+            pltpu.VMEM((nf, rows, cols), jnp.bfloat16),
+            pltpu.VMEM(tokens.shape, jnp.bfloat16),
+            pltpu.VMEM((count, cols), F32),
+            dma((4, 16)),
+            dma((4,)),
+            dma((16,)),
+            dma((4,)),
+            dma(()),
+            dma(()),
+        ],
+        compiler_params=pltpu.CompilerParams(
+            collective_id=1, has_side_effects=True, vmem_limit_bytes=60 * 1024 * 1024
+        ),
+    )(tokens, new_weight)
+
+
 def local(nf, nt, tokens, weight, momentum, gradient, probes):
     moment = 0.9 * momentum + gradient.astype(F32)
     krylov, scale = lanczos(probes, moment, nf, nt)
     new_weight = (weight.astype(F32) - moment * scale[0, 0]).astype(jnp.bfloat16)
-    summed = jnp.dot(
-        tokens,
-        lax.all_gather(new_weight, "fsdp", axis=0, tiled=True),
-        preferred_element_type=F32,
-    )
+    summed = gather_multiply(tokens, new_weight, nf, nt)
     size = STEPS * K
     return (summed, moment, krylov[:size, :size])
 

time: 249 us -> 198 us (0.80)
  waiting for transfers between devices: 111 us -> 0 us
  Pallas kernels: 76.8 us -> 185 us
  matrix products: 35.2 us -> 0 us
  between operations: 14.1 us -> 0.69 us
    all_gather x1 -> x0, waiting for transfers between devices: 111 us -> none  [local(): lax.all_gather(new_weight, 'fsdp', axis=0, tiled=True)]
    pallas_call x0 -> x1, Pallas kernels: none -> 108 us  [gather_multiply(): pl.pallas_call(functools.partial(gather_kernel, nt), out_shape=jax.ShapeD...]
    dot_general x1 -> x0, matrix products: 35.2 us -> none  [local(): jnp.dot(tokens, lax.all_gather(new_weight, 'fsdp', axis=0, tiled=True), p...]
  transfers between devices with their start and end apart: 1 -> 0, of which waited for: 1 -> 0; matrix products, arithmetic and copies ran while one was open for 0% -> 0% of each run, Pallas kernels for 0% -> 0%
where the time goes in v3:
time: 198 us; the launch traced here: 197 us
  Pallas kernels  185 us (93%)
  local copies, waits for them, and re-layouts  7.47 us (4%)
  other arithmetic  4.15 us (2%)
    pallas_call x1, Pallas kernels, gather_multiply(): pl.pallas_call(functools.partial(gather_kernel, nt), out_shape=jax.ShapeD...  108 us
    pallas_call x1, Pallas kernels, lanczos(): pl.pallas_call(functools.partial(lanczos_kernel, nf, nt), out_shape=(jax....  76.8 us
    unnamed x7, local copies, waits for them, and re-layouts  6.3 us

profile of v3, /device:TPU:1, one launch (start us, length us, event | category | flops | bytes accessed | tf_op | source)
XLA Modules:
  0.0 196.9 jit_solution(15807115855261654236)
XLA Ops:
  0.6 0.0 copy-start.1
  0.6 2.2 %convert_add_fusion.moment_ref = f32[256,2048]{1,0:T(8,128)S(1)} fusion(bf16[256,2048]{1,0:T(8,128)(2,1)} %param.8, f32[256,2048]{1,0:T(8,128)} %param.7), kind=kLoop, calls=%fused_computation.1 | loop fusion | flops 1572864 | bytes 5242880 | tf_op jit(solution)/shard_map/add | solution.py:475
  2.9 0.0 copy-done.1
  2.9 0.0 copy-start
  2.9 0.0 copy-start.2
  2.9 76.8 %shard_map.76 = (f32[128,128]{1,0:T(8,128)S(1)}, f32[8,128]{1,0:T(8,128)S(1)}) custom-call(f32[32,2048]{1,0:T(8,128)S(1)} %copy-done.1, f32[256,2048]{1,0:T(8,128)S(1)} %convert_add_fusion.moment_ref), custom_call_target="tpu_custom_call" | custom-call | tf_op jit(solution)/shard_map/pallas_call | solution.py:265
  79.8 0.5 slice.6
  80.3 0.6 slice.7
  80.9 0.0 copy-done.2
  80.9 1.9 subtract_convert_fusion.new_ref
  82.8 0.0 copy-done
  82.8 107.8 %shard_map.77 = f32[768,2048]{1,0:T(8,128)} custom-call(bf16[768,8192]{1,0:T(8,128)(2,1)} %tokens_ref.1, bf16[256,2048]{1,0:T(8,128)(2,1)} %subtract_convert_fusion.new_ref), custom_call_target="tpu_custom_call" | custom-call | tf_op jit(solution)/shard_map/pallas_call | solution.py:452
  190.7 6.3 %copy.9 = f32[768,2048]{1,0:T(8,128)} copy(f32[768,2048]{1,0:T(8,128)} %shard_map.77) | data formatting | bytes 12582912
Async XLA Ops:
  0.6 2.3 %copy-start.1 = (f32[32,2048]{1,0:T(8,128)S(1)}, f32[32,2048]{1,0:T(8,128)}, u32[]{:S(2)}) copy-start(f32[32,2048]{1,0:T(8,128)} %probes_ref.1) | copy-start | bytes 786436
  2.9 79.9 %copy-start = (f32[256,2048]{1,0:T(8,128)}, f32[256,2048]{1,0:T(8,128)S(1)}, u32[]{:S(2)}) copy-start(f32[256,2048]{1,0:T(8,128)S(1)} %convert_add_fusion.moment_ref) | copy-start | bytes 6291460
  2.9 78.0 %copy-start.2 = (bf16[256,2048]{1,0:T(8,128)(2,1)S(1)}, bf16[256,2048]{1,0:T(8,128)(2,1)}, u32[]{:S(2)}) copy-start(bf16[256,2048]{1,0:T(8,128)(2,1)} %param.6) | copy-start | bytes 3145732

commit v4 on v2

--- a/solution.py
+++ b/solution.py
@@ -85,13 +85,138 @@
     return jnp.sum(krylov * (down * along)) / length
 
 
-def lanczos_kernel(
+def signed(n):
+    return (n + 1) % 4 - 1
+
+
+def mod4(at):
+    return at[0] % 4, at[1] % 4
+
+
+PIECES = (("a", 1), ("a", -1), ("b", 1), ("b", -1))
+GROUPS = (
+    ((1, 0), (0, 1)),
+    ((-1, 0), (0, -1)),
+    ((1, 1), (-1, -1)),
+    ((1, -1), (-1, 1)),
+    ((2, 0), (0, 2)),
+    ((2, 1), (1, 2)),
+    ((2, -1), (-1, 2)),
+    ((2, 2),),
+)
+
+
+def onward(piece, source):
+    first, sign = piece
+    u, v = signed(-source[0]), signed(-source[1])
+    if first == "b":
+        u, v = v, u
+    out = []
+    if v == 0:
+        if u == 0:
+            out += [(1, 0), (-1, 0)]
+        elif u == sign:
+            out += [(sign, 0)]
+        out += [(0, 1), (0, -1)]
+    elif v == sign:
+        out += [(0, sign)]
+    if first == "b":
+        out = [(v, u) for u, v in out]
+    return out
+
+
+def slot(at):
+    i, j = mod4(at)
+    return 4 * i + j
+
+
+def spans(start, counts):
+    out = []
+    for count in counts:
+        out.append((start, start + count))
+        start += count
+    return tuple(out)
+
+
+EARLY = spans(0, (32, 32, 16, 16))
+LATE = spans(96, (32, 32, 48, 48))
+DURING_TENSOR = ((), (1,), (4,))
+DURING_SCATTER = ((), (2,))
+DURING_GATHER = ((0,), (3,))
+DURING_LAST = (5,)
+AFTER = (6, 7)
+
+
+class Flow:
+    def __init__(self, wall, mall, rows, recv, send, sib_recv, sib_send, device_at, sibling):
+        self.wall, self.mall, self.rows = wall, mall, rows
+        self.recv, self.send, self.sib_recv, self.sib_send = recv, send, sib_recv, sib_send
+        self.device_at, self.sibling = device_at, sibling
+        self.first, self.last = rows[0][0], rows[-1][1]
+        self.kinds = 2 if mall is not None else 1
+
+    def copies(self, owner, low, high, send, recv, to):
+        band = pl.ds(low, high - low)
+        for ref in (self.wall, self.mall)[: self.kinds]:
+            pltpu.make_async_remote_copy(
+                src_ref=ref.at[owner, band],
+                dst_ref=ref.at[owner, band],
+                send_sem=send,
+                recv_sem=recv,
+                device_id=to,
+            ).start()
+
+    def bytes_of(self, count, high_less_low, sem):
+        ref = self.wall.at[pl.ds(0, count), pl.ds(0, self.kinds * high_less_low)]
+        return pltpu.make_async_remote_copy(
+            src_ref=ref, dst_ref=ref, send_sem=sem, recv_sem=sem, device_id=self.sibling
+        )
+
+    def pass_on(self, t, owner, source, to):
+        low, high = self.rows[t]
+        there = self.recv.at[t, slot((source[0] - to[0], source[1] - to[1]))]
+        self.copies(owner, low, high, self.send.at[t], there, self.device_at(to))
+
+    def to_sibling(self, owner, source):
+        there = self.sib_recv.at[slot((source[1], source[0]))]
+        self.copies(owner, self.first, self.last, self.sib_send, there, self.sibling)
+
+    def begin(self, owner):
+        for rank in range(4):
+            for t, piece in enumerate(PIECES):
+                self.pass_on(t, owner, (0, 0), onward(piece, (0, 0))[rank])
+        self.to_sibling(owner, (0, 0))
+
+    def events(self, owner, source):
+        for t, piece in enumerate(PIECES):
+            low, high = self.rows[t]
+            self.bytes_of(1, high - low, self.recv.at[t, slot(source)]).wait_recv()
+            for to in onward(piece, source):
+                self.pass_on(t, owner, source, to)
+        self.to_sibling(owner, source)
+
+    def from_sibling(self, owner, source):
+        self.bytes_of(1, self.last - self.first, self.sib_recv.at[slot(source)]).wait_recv()
+
+    def sent(self):
+        for t, (low, high) in enumerate(self.rows):
+            self.bytes_of(15, high - low, self.send.at[t]).wait_send()
+        self.bytes_of(16, self.last - self.first, self.sib_send).wait_send()
+
+
+def step_kernel(
     nf,
     nt,
+    tokens_ref,
+    weight_ref,
     probes_ref,
     moment_ref,
+    out_ref,
     krylov_ref,
-    scale_ref,
+    wall,
+    mall,
+    acc,
+    toks,
     block,
     basis,
     small,
@@ -100,6 +225,16 @@
     frecv,
     gathered,
     drecv,
+    early_recv,
+    early_send,
+    early_sib_recv,
+    early_sib_send,
+    late_recv,
+    late_send,
+    late_sib_recv,
+    late_sib_send,
+    tok_sem,
+    out_sem,
     t_send,
     t_recv,
     rs_send,
@@ -111,9 +246,22 @@
 ):
     mf = lax.axis_index("fsdp")
     mt = lax.axis_index("tensor")
-    rows = moment_ref.shape[0]
-    cols = moment_ref.shape[1]
+    rows, cols = moment_ref.shape
     width = cols // 8
+    core = lax.rem(mf, 2)
+    chip = lax.div(mf, 2)
+    mx, mz = lax.div(chip, 4), lax.rem(chip, 4)
+
+    def chip_at(at):
+        i, j = at
+        x = lax.rem(mx + 4 + i * (1 - core) + j * core, 4)
+        z = lax.rem(mz + 4 + i * core + j * (1 - core), 4)
+        return 4 * x + z
+
+    def device_at(at):
+        return {"fsdp": 2 * chip_at(at) + core}
+
+    sibling = {"fsdp": 2 * chip + 1 - core}
 
     def fsdp_at(k):
         return {"fsdp": lax.rem(mf + k, nf)}
@@ -153,6 +301,20 @@
             device_id=fsdp_at(1),
         )
 
+    early = Flow(wall, mall, EARLY, early_recv, early_send, early_sib_recv, early_sib_send, device_at, sibling)
+    late = Flow(wall, None, LATE, late_recv, late_send, late_sib_recv, late_sib_send, device_at, sibling)
+    ahead = EARLY[-1][1]
+
+    def owner_at(source):
+        return 2 * chip_at(source) + core
+
+    def early_events(*numbers):
+        for number in numbers:
+            for source in GROUPS[number]:
+                early.events(owner_at(source), source)
+
+    wall[mf, :ahead] = weight_ref[:ahead]
+    mall[mf] = moment_ref[:ahead].astype(jnp.bfloat16)
     block[...] = probes_ref[...]
     small[...] = jnp.zeros_like(small)
     upper = None
@@ -176,6 +338,9 @@
                 device_id=tensor_at(k),
             ).start()
 
+        if step == 0:
+            early.begin(mf)
+        early_events(*DURING_TENSOR[step])
         all_of(tbuf.at[step], t_send.at[step], t_recv.at[step], nt - 1).wait_recv()
         total = tbuf[step, 0]
         for other in range(1, nt):
@@ -203,6 +368,7 @@
                 rs_recv.at[step],
             )
             basis[step] = hdot(inverse_low, now)
+            early_events(*DURING_SCATTER[step])
             all_of(frecv.at[step], rs_send.at[step], rs_recv.at[step], nf - 1).wait_recv()
             summed = jnp.sum(frecv[step], axis=0)
             gathered[step, mf] = summed[:, :width]
@@ -217,6 +383,7 @@
             if step:
                 rest = rest + hdot(upper_next[:, :K], basis[step - 1])
             block[...] = rest
+            early_events(*DURING_GATHER[step])
             all_of(gathered.at[step], ag_send.at[step], ag_recv.at[step], nf - 1).wait_recv()
             for r in range(4):
                 for c in range(8):
@@ -225,6 +392,7 @@
         else:
             drecv[mf] = tile
             to_all(lambda dest: drecv.at[mf], drecv.at[mf], d_send, d_recv)
+            early_events(*DURING_LAST)
             all_of(drecv, d_send, d_recv, nf - 1).wait_recv()
             diag = unpack(jnp.sum(drecv[...], axis=0))
         diags.append(diag)
@@ -247,30 +415,94 @@
     krylov = jnp.concatenate(bands, axis=0)
     top = top_value(krylov)
     krylov_ref[...] = krylov / top
-    scale_ref[...] = jnp.full(scale_ref.shape, 1.0, F32) / jnp.sqrt(top)
-
+    scale = 1.0 / jnp.sqrt(top)
+    fresh = weight_ref[ahead:].astype(F32) - moment_ref[ahead:] * scale
+    wall[mf, ahead:] = fresh.astype(jnp.bfloat16)
+    late.begin(mf)
+
+    early_events(*AFTER)
+    early.sent()
+
+    order = [(0, 0)] + [source for group in GROUPS for source in group]
+
+    def tokens_of(number):
+        columns = pl.ds(pl.multiple_of(chip_at(order[number]) * 2 * rows, 2 * rows), 2 * rows)
+        return pltpu.make_async_copy(
+            tokens_ref.at[:, columns], toks.at[number % 2], tok_sem.at[number % 2]
+        )
+
+    tokens_of(0).start()
+
+    def multiply(source):
+        number = order.index(source)
+        if number + 1 < len(order):
+            tokens_of(number + 1).start()
+        left_owner = 2 * chip_at(source)
+        early.from_sibling(left_owner + 1 - core, source)
+        for at in range(2):
+
+            @pl.loop(0, ahead // 16)
+            def _(n):
+                band = pl.ds(pl.multiple_of(n * 16, 16), 16)
+                value = wall[left_owner + at, band].astype(F32)
+                value = value - mall[left_owner + at, band].astype(F32) * scale
+                wall[left_owner + at, band] = value.astype(jnp.bfloat16)
+
+        late.from_sibling(left_owner + 1 - core, source)
+        tokens_of(number).wait()
+        left = toks[number % 2]
+
+        @pl.loop(0, cols // 512)
+        def _(n):
+            at = pl.ds(pl.multiple_of(n * 512, 512), 512)
+            right = wall[pl.ds(left_owner, 2), :, at].reshape(2 * rows, 512)
+            product = jnp.dot(left, right, preferred_element_type=F32)
+            if number:
+                acc[:, at] += product
+            else:
+                acc[:, at] = product
+
+    before = ((0, 0),)
+    for group in GROUPS:
+        for source in group:
+            late.events(owner_at(source), source)
+        for source in before:
+            multiply(source)
+        before = group
+    for source in before:
+        multiply(source)
+    copy = pltpu.make_async_copy(acc, out_ref, out_sem)
+    copy.start()
+    late.sent()
     for step in range(STEPS):
         all_of(tbuf.at[step], t_send.at[step], t_recv.at[step], nt - 1).wait_send()
         if step + 1 < STEPS:
             all_of(fsend.at[step], rs_send.at[step], rs_recv.at[step], nf - 1).wait_send()
             all_of(gathered.at[step], ag_send.at[step], ag_recv.at[step], nf - 1).wait_send()
     all_of(drecv, d_send, d_recv, nf - 1).wait_send()
-
-
-def lanczos(probes, moment, nf, nt):
+    copy.wait()
+
+
+def step_call(tokens, weight, probes, moment, nf, nt):
     rows, cols = moment.shape
     width = cols // 8
+    count = tokens.shape[0]
     vmem = pl.BlockSpec(memory_space=pltpu.VMEM)
+    anywhere = pl.BlockSpec(memory_space=pl.ANY)
     dma = pltpu.SemaphoreType.DMA
     return pl.pallas_call(
-        functools.partial(lanczos_kernel, nf, nt),
+        functools.partial(step_kernel, nf, nt),
         out_shape=(
+            jax.ShapeDtypeStruct((count, cols), F32),
             jax.ShapeDtypeStruct((LANES, LANES), F32),
-            jax.ShapeDtypeStruct((8, LANES), F32),
         ),
-        in_specs=[vmem, vmem],
-        out_specs=(vmem, vmem),
+        in_specs=[anywhere, vmem, vmem, vmem],
+        out_specs=(anywhere, vmem),
         scratch_shapes=[
+            pltpu.VMEM((nf, rows, cols), jnp.bfloat16),
+            pltpu.VMEM((nf, EARLY[-1][1], cols), jnp.bfloat16),
+            pltpu.VMEM((count, cols), F32),
+            pltpu.VMEM((2, count, 2 * rows), jnp.bfloat16),
             pltpu.VMEM((K, cols), F32),
             pltpu.VMEM((STEPS - 1, K, cols), F32),
             pltpu.VMEM((K, LANES), F32),
@@ -279,6 +511,16 @@
             pltpu.VMEM((STEPS - 1, nf, 8, width + LANES), F32),
             pltpu.VMEM((STEPS - 1, nf, 8, width), F32),
             pltpu.VMEM((nf, 8, LANES), F32),
+            dma((4, 16)),
+            dma((4,)),
+            dma((16,)),
+            dma(()),
+            dma((4, 16)),
+            dma((4,)),
+            dma((16,)),
+            dma(()),
+            dma((2,)),
+            dma(()),
             dma((STEPS,)),
             dma((STEPS,)),
             dma((STEPS - 1,)),
@@ -289,20 +531,14 @@
             dma(()),
         ],
         compiler_params=pltpu.CompilerParams(
-            collective_id=0, has_side_effects=True, vmem_limit_bytes=40 * 1024 * 1024
+            collective_id=0, has_side_effects=True, vmem_limit_bytes=62 * 1024 * 1024
         ),
-    )(probes, moment)
+    )(tokens, weight, probes, moment)
 
 
 def local(nf, nt, tokens, weight, momentum, gradient, probes):
     moment = 0.9 * momentum + gradient.astype(F32)
-    krylov, scale = lanczos(probes, moment, nf, nt)
-    new_weight = (weight.astype(F32) - moment * scale[0, 0]).astype(jnp.bfloat16)
-    summed = jnp.dot(
-        tokens,
-        lax.all_gather(new_weight, "fsdp", axis=0, tiled=True),
-        preferred_element_type=F32,
-    )
+    summed, krylov = step_call(tokens, weight, probes, moment, nf, nt)
     size = STEPS * K
     return (summed, moment, krylov[:size, :size])
 

time: 249 us -> 203 us (0.82)
  Pallas kernels: 76.8 us -> 191 us
  waiting for transfers between devices: 111 us -> 0 us
  matrix products: 35.2 us -> 0 us
  between operations: 14.1 us -> 0.64 us
    pallas_call x1, Pallas kernels: 76.8 us -> 191 us  [step_call(): pl.pallas_call(functools.partial(step_kernel, nf, nt), out_shape=(jax.Sha...]
    all_gather x1 -> x0, waiting for transfers between devices: 111 us -> none  [local(): lax.all_gather(new_weight, 'fsdp', axis=0, tiled=True)]
    dot_general x1 -> x0, matrix products: 35.2 us -> none  [local(): jnp.dot(tokens, lax.all_gather(new_weight, 'fsdp', axis=0, tiled=True), p...]
    unnamed x7 -> x1, local copies, waits for them, and re-layouts: 6.58 us -> 6.28 us
  transfers between devices with their start and end apart: 1 -> 0, of which waited for: 1 -> 0; matrix products, arithmetic and copies ran while one was open for 0% -> 0% of each run, Pallas kernels for 0% -> 0%
where the time goes in v4:
time: 203 us; the launch traced here: 202 us
  Pallas kernels  191 us (94%)
  local copies, waits for them, and re-layouts  7.71 us (4%)
  other arithmetic  3.63 us (2%)
    pallas_call x1, Pallas kernels, step_call(): pl.pallas_call(functools.partial(step_kernel, nf, nt), out_shape=(jax.Sha...  191 us
    unnamed x1, local copies, waits for them, and re-layouts  6.28 us

profile of v4, /device:TPU:1, one launch (start us, length us, event | category | flops | bytes accessed | tf_op | source)
XLA Modules:
  0.0 202.5 jit_solution(8828616967718353380)
XLA Ops:
  0.6 3.6 %convert_add_fusion.moment_ref = f32[256,2048]{1,0:T(8,128)} fusion(bf16[256,2048]{1,0:T(8,128)(2,1)} %param.8, f32[256,2048]{1,0:T(8,128)} %param.7), kind=kLoop, calls=%fused_computation | loop fusion | flops 1572864 | bytes 5242880 | tf_op jit(solution)/shard_map/add | solution.py:540
  4.3 190.5 %shard_map.76 = (f32[768,2048]{1,0:T(8,128)}, f32[128,128]{1,0:T(8,128)}) custom-call(bf16[768,8192]{1,0:T(8,128)(2,1)} %tokens_ref.1, bf16[256,2048]{1,0:T(8,128)(2,1)} %weight_ref.1, f32[32,2048]{1,0:T(8,128)} %probes_ref.1, f32[256,2048]{1,0:T(8,128)} %convert_add_fusion.moment_ref), custom_call_target="tpu_custom_call" | custom-call | tf_op jit(solution)/shard_map/pallas_call | solution.py:493
  194.8 1.4 slice.3
  196.2 6.3 %copy.9 = f32[768,2048]{1,0:T(8,128)} copy(f32[768,2048]{1,0:T(8,128)} %get-tuple-element.10) | data formatting | bytes 12582912

commit v5 on v4

--- a/solution.py
+++ b/solution.py
@@ -22,6 +22,25 @@
     return lax.dot_general(
         left, right, (((1,), (1,)), ((), ())), precision=HIGHEST, preferred_element_type=F32
     )
+
+
+def split(value):
+    high = value.astype(jnp.bfloat16)
+    rest = value - high.astype(F32)
+    middle = rest.astype(jnp.bfloat16)
+    return high, middle, (rest - middle.astype(F32)).astype(jnp.bfloat16)
+
+
+def split_dot(left, right, contract):
+    def dot(a, b):
+        return lax.dot_general(a, b, (((1,), (contract,)), ((), ())), preferred_element_type=F32)
+
+    high, middle, low = split(left)
+    first = dot(jnp.concatenate([high, middle, low], axis=0), right[0])
+    second = dot(jnp.concatenate([high, middle], axis=0), right[1])
+    third = dot(high, right[2])
+    small = first[2 * K :] + second[K:] + third
+    return first[:K] + ((first[K : 2 * K] + second[:K]) + small)
 
 
 def eliminate(gram):
@@ -138,13 +157,10 @@
     return tuple(out)
 
 
-EARLY = spans(0, (32, 32, 16, 16))
-LATE = spans(96, (32, 32, 48, 48))
-DURING_TENSOR = ((), (1,), (4,))
-DURING_SCATTER = ((), (2,))
-DURING_GATHER = ((0,), (3,))
-DURING_LAST = (5,)
-AFTER = (6, 7)
+EARLY = spans(0, (16, 16, 16, 16))
+LATE = spans(64, (48, 48, 48, 48))
+DURING_TENSOR = ((), (0, 1), (2, 3, 4))
+AFTER = (5, 6, 7)
 
 
 class Flow:
@@ -210,8 +226,10 @@
     tokens_ref,
     weight_ref,
     probes_ref,
-    moment_ref,
-    out_ref,
+    momentum_ref,
+    gradient_ref,
+    partial_ref,
+    last_ref,
     krylov_ref,
     wall,
     mall,
@@ -220,6 +238,8 @@
     block,
     basis,
     small,
+    parts,
+    gbuf,
     tbuf,
     fsend,
     frecv,
@@ -235,6 +255,8 @@
     late_sib_send,
     tok_sem,
     out_sem,
+    g_send,
+    g_recv,
     t_send,
     t_recv,
     rs_send,
@@ -246,7 +268,7 @@
 ):
     mf = lax.axis_index("fsdp")
     mt = lax.axis_index("tensor")
-    rows, cols = moment_ref.shape
+    rows, cols = momentum_ref.shape
     width = cols // 8
     core = lax.rem(mf, 2)
     chip = lax.div(mf, 2)
@@ -292,6 +314,16 @@
                 device_id=fsdp_at(k),
             ).start()
 
+    def to_tensor(ref, send, recv):
+        for k in range(1, nt):
+            pltpu.make_async_remote_copy(
+                src_ref=ref,
+                dst_ref=ref,
+                send_sem=send,
+                recv_sem=recv,
+                device_id=tensor_at(k),
+            ).start()
+
     def all_of(ref, send, recv, count):
         return pltpu.make_async_remote_copy(
             src_ref=ref.at[pl.ds(0, count)],
@@ -313,53 +345,55 @@
             for source in GROUPS[number]:
                 early.events(owner_at(source), source)
 
-    wall[mf, :ahead] = weight_ref[:ahead]
-    mall[mf] = moment_ref[:ahead].astype(jnp.bfloat16)
     block[...] = probes_ref[...]
     small[...] = jnp.zeros_like(small)
-    upper = None
+
+    def send_gram(step, now):
+        small[:, :K] = hdot_t(now, now)
+        gbuf[step, mt] = pack(small[...])
+        if step == 0:
+            pl.semaphore_wait(barrier, nf + nt - 2)
+        to_tensor(gbuf.at[step, mt], g_send.at[step], g_recv.at[step])
+
+    send_gram(0, probes_ref[...])
+    moment = 0.9 * momentum_ref[...] + gradient_ref[...].astype(F32)
+    for at, value in enumerate(split(moment)):
+        parts[at] = value
+    wall[mf, :ahead] = weight_ref[:ahead]
+    mall[mf] = parts[0, :ahead]
     diags, uppers = [], []
     for step in range(STEPS):
         now = block[...]
-        mine = tbuf.at[step, mt]
-        mine[:, rows:] = jnp.zeros((K, LANES), F32)
-        mine[:, :rows] = hdot_t(now, moment_ref[...])
-        mine[:, rows : rows + K] = hdot_t(now, now)
-        if step == 0:
-            pl.semaphore_wait(barrier, nf + nt - 2)
-
-        @pl.loop(1, nt)
-        def _(k):
-            pltpu.make_async_remote_copy(
-                src_ref=tbuf.at[step, mt],
-                dst_ref=tbuf.at[step, mt],
-                send_sem=t_send.at[step],
-                recv_sem=t_recv.at[step],
-                device_id=tensor_at(k),
-            ).start()
-
+        if step:
+            send_gram(step, now)
+        tbuf[step, mt] = split_dot(now, parts, 1)
+        to_tensor(tbuf.at[step, mt], t_send.at[step], t_recv.at[step])
         if step == 0:
             early.begin(mf)
+        all_of(gbuf.at[step], g_send.at[step], g_recv.at[step], nt - 1).wait_recv()
+        gram = gbuf[step, 0]
+        for other in range(1, nt):
+            gram = gram + gbuf[step, other]
+        upper_next, inverse_low = eliminate(unpack(gram))
+        if step:
+            uppers.append(upper_next)
         early_events(*DURING_TENSOR[step])
         all_of(tbuf.at[step], t_send.at[step], t_recv.at[step], nt - 1).wait_recv()
         total = tbuf[step, 0]
         for other in range(1, nt):
             total = total + tbuf[step, other]
-        upper_next, inverse_low = eliminate(total[:, rows:])
-        if step:
-            uppers.append(upper_next)
         inverse_low = inverse_low[:, :K]
-        reduced = hdot(inverse_low, total[:, :rows])
+        reduced = hdot(inverse_low, total)
         small[:, :K] = hdot_t(reduced, reduced)
         tile = pack(small[...])
         if step + 1 < STEPS:
-            images = hdot(reduced, moment_ref[...])
+            drecv[step, mf] = tile
+            images = split_dot(reduced, parts, 0)
             for r in range(4):
                 for c in range(8):
-                    fsend[step, 8 * r + c, :, :width] = images[
+                    fsend[step, 8 * r + c] = images[
                         8 * r : 8 * r + 8, width * c : width * (c + 1)
                     ]
-                    fsend[step, 8 * r + c, :, width:] = tile
             frecv[step, mf] = fsend[step, mf]
             to_all(
                 lambda dest: fsend.at[step, dest],
@@ -367,34 +401,37 @@
                 rs_send.at[step],
                 rs_recv.at[step],
             )
+            to_all(
+                lambda dest: drecv.at[step, mf], drecv.at[step, mf], d_send.at[step], d_recv.at[step]
+            )
             basis[step] = hdot(inverse_low, now)
-            early_events(*DURING_SCATTER[step])
             all_of(frecv.at[step], rs_send.at[step], rs_recv.at[step], nf - 1).wait_recv()
             summed = jnp.sum(frecv[step], axis=0)
-            gathered[step, mf] = summed[:, :width]
+            gathered[step, mf] = summed
             to_all(
                 lambda dest: gathered.at[step, mf],
                 gathered.at[step, mf],
                 ag_send.at[step],
                 ag_recv.at[step],
             )
-            diag = unpack(summed[:, width:])
+            all_of(drecv.at[step], d_send.at[step], d_recv.at[step], nf - 1).wait_recv()
+            diag = unpack(jnp.sum(drecv[step], axis=0))
             rest = hdot(diag[:, :K], basis[step])
             if step:
                 rest = rest + hdot(upper_next[:, :K], basis[step - 1])
             block[...] = rest
-            early_events(*DURING_GATHER[step])
             all_of(gathered.at[step], ag_send.at[step], ag_recv.at[step], nf - 1).wait_recv()
             for r in range(4):
                 for c in range(8):
                     where = (slice(8 * r, 8 * r + 8), slice(width * c, width * (c + 1)))
                     block[where] = gathered[step, 8 * r + c] - block[where]
         else:
-            drecv[mf] = tile
-            to_all(lambda dest: drecv.at[mf], drecv.at[mf], d_send, d_recv)
-            early_events(*DURING_LAST)
-            all_of(drecv, d_send, d_recv, nf - 1).wait_recv()
-            diag = unpack(jnp.sum(drecv[...], axis=0))
+            drecv[step, mf] = tile
+            to_all(
+                lambda dest: drecv.at[step, mf], drecv.at[step, mf], d_send.at[step], d_recv.at[step]
+            )
+            all_of(drecv.at[step], d_send.at[step], d_recv.at[step], nf - 1).wait_recv()
+            diag = unpack(jnp.sum(drecv[step], axis=0))
         diags.append(diag)
 
     eye = jnp.where(lax.broadcasted_iota(jnp.int32, (K, K), 0) == lax.broadcasted_iota(jnp.int32, (K, K), 1), 1.0, 0.0)
@@ -416,7 +453,8 @@
     top = top_value(krylov)
     krylov_ref[...] = krylov / top
     scale = 1.0 / jnp.sqrt(top)
-    fresh = weight_ref[ahead:].astype(F32) - moment_ref[ahead:] * scale
+    fresh = 0.9 * momentum_ref[ahead:] + gradient_ref[ahead:].astype(F32)
+    fresh = weight_ref[ahead:].astype(F32) - fresh * scale
     wall[mf, ahead:] = fresh.astype(jnp.bfloat16)
     late.begin(mf)
 
@@ -433,21 +471,24 @@
 
     tokens_of(0).start()
 
-    def multiply(source):
-        number = order.index(source)
-        if number + 1 < len(order):
-            tokens_of(number + 1).start()
-        left_owner = 2 * chip_at(source)
-        early.from_sibling(left_owner + 1 - core, source)
+    def combine(source):
+        owner = 2 * chip_at(source)
+        early.from_sibling(owner + 1 - core, source)
         for at in range(2):
 
             @pl.loop(0, ahead // 16)
             def _(n):
                 band = pl.ds(pl.multiple_of(n * 16, 16), 16)
-                value = wall[left_owner + at, band].astype(F32)
-                value = value - mall[left_owner + at, band].astype(F32) * scale
-                wall[left_owner + at, band] = value.astype(jnp.bfloat16)
-
+                value = wall[owner + at, band].astype(F32)
+                value = value - mall[owner + at, band].astype(F32) * scale
+                wall[owner + at, band] = value.astype(jnp.bfloat16)
+
+    def multiply(source):
+        number = order.index(source)
+        if number + 2 < len(order):
+            tokens_of(number + 1).start()
+        left_owner = 2 * chip_at(source)
+        combine(source)
         late.from_sibling(left_owner + 1 - core, source)
         tokens_of(number).wait()
         left = toks[number % 2]
@@ -463,7 +504,7 @@
                 acc[:, at] = product
 
     before = ((0, 0),)
-    for group in GROUPS:
+    for group in GROUPS[:-1]:
         for source in group:
             late.events(owner_at(source), source)
         for source in before:
@@ -471,20 +512,28 @@
         before = group
     for source in before:
         multiply(source)
-    copy = pltpu.make_async_copy(acc, out_ref, out_sem)
-    copy.start()
+    partial = pltpu.make_async_copy(acc, partial_ref, out_sem)
+    partial.start()
+    last = GROUPS[-1][0]
+    combine(last)
+    late.events(owner_at(last), last)
+    late.from_sibling(2 * chip_at(last) + 1 - core, last)
+    final = pltpu.make_async_copy(wall.at[pl.ds(2 * chip_at(last), 2)], last_ref, tok_sem.at[0])
+    final.start()
     late.sent()
     for step in range(STEPS):
+        all_of(gbuf.at[step], g_send.at[step], g_recv.at[step], nt - 1).wait_send()
         all_of(tbuf.at[step], t_send.at[step], t_recv.at[step], nt - 1).wait_send()
+        all_of(drecv.at[step], d_send.at[step], d_recv.at[step], nf - 1).wait_send()
         if step + 1 < STEPS:
             all_of(fsend.at[step], rs_send.at[step], rs_recv.at[step], nf - 1).wait_send()
             all_of(gathered.at[step], ag_send.at[step], ag_recv.at[step], nf - 1).wait_send()
-    all_of(drecv, d_send, d_recv, nf - 1).wait_send()
-    copy.wait()
-
-
-def step_call(tokens, weight, probes, moment, nf, nt):
-    rows, cols = moment.shape
+    partial.wait()
+    final.wait()
+
+
+def step_call(tokens, weight, momentum, gradient, probes, nf, nt):
+    rows, cols = momentum.shape
     width = cols // 8
     count = tokens.shape[0]
     vmem = pl.BlockSpec(memory_space=pltpu.VMEM)
@@ -494,10 +543,11 @@
         functools.partial(step_kernel, nf, nt),
         out_shape=(
             jax.ShapeDtypeStruct((count, cols), F32),
+            jax.ShapeDtypeStruct((2, rows, cols), jnp.bfloat16),
             jax.ShapeDtypeStruct((LANES, LANES), F32),
         ),
-        in_specs=[anywhere, vmem, vmem, vmem],
-        out_specs=(anywhere, vmem),
+        in_specs=[anywhere, vmem, vmem, vmem, vmem],
+        out_specs=(anywhere, anywhere, vmem),
         scratch_shapes=[
             pltpu.VMEM((nf, rows, cols), jnp.bfloat16),
             pltpu.VMEM((nf, EARLY[-1][1], cols), jnp.bfloat16),
@@ -506,11 +556,13 @@
             pltpu.VMEM((K, cols), F32),
             pltpu.VMEM((STEPS - 1, K, cols), F32),
             pltpu.VMEM((K, LANES), F32),
-            pltpu.VMEM((STEPS, nt, K, rows + LANES), F32),
-            pltpu.VMEM((STEPS - 1, nf, 8, width + LANES), F32),
-            pltpu.VMEM((STEPS - 1, nf, 8, width + LANES), F32),
+            pltpu.VMEM((3, rows, cols), jnp.bfloat16),
+            pltpu.VMEM((STEPS, nt, 8, LANES), F32),
+            pltpu.VMEM((STEPS, nt, K, rows), F32),
             pltpu.VMEM((STEPS - 1, nf, 8, width), F32),
-            pltpu.VMEM((nf, 8, LANES), F32),
+            pltpu.VMEM((STEPS - 1, nf, 8, width), F32),
+            pltpu.VMEM((STEPS - 1, nf, 8, width), F32),
+            pltpu.VMEM((STEPS, nf, 8, LANES), F32),
             dma((4, 16)),
             dma((4,)),
             dma((16,)),
@@ -523,24 +575,76 @@
             dma(()),
             dma((STEPS,)),
             dma((STEPS,)),
+            dma((STEPS,)),
+            dma((STEPS,)),
             dma((STEPS - 1,)),
             dma((STEPS - 1,)),
             dma((STEPS - 1,)),
             dma((STEPS - 1,)),
-            dma(()),
-            dma(()),
+            dma((STEPS,)),
+            dma((STEPS,)),
         ],
         compiler_params=pltpu.CompilerParams(
-            collective_id=0, has_side_effects=True, vmem_limit_bytes=62 * 1024 * 1024
+            collective_id=0, has_side_effects=True, vmem_limit_bytes=63 * 1024 * 1024
         ),
-    )(tokens, weight, probes, moment)
+    )(tokens, weight, probes, momentum, gradient)
+
+
+def finish_kernel(
+    chip_ref,
+    partial_ref,
+    tokens_ref,
+    last_ref,
+    momentum_ref,
+    gradient_ref,
+    krylov_ref,
+    out_ref,
+    moment_ref,
+    scaled_ref,
+):
+    both, rows, cols = last_ref.shape
+    right = last_ref[...].reshape(both * rows, cols)
+    out_ref[...] = partial_ref[...] + jnp.dot(tokens_ref[...], right, preferred_element_type=F32)
+    moment_ref[...] = 0.9 * momentum_ref[...] + gradient_ref[...].astype(F32)
+    size = scaled_ref.shape[0]
+    scaled_ref[...] = krylov_ref[:size, :size]
+
+
+def finish(chip, partial, tokens, last, momentum, gradient, krylov):
+    count, cols = partial.shape
+    rows = momentum.shape[0]
+    turns = 8
+    size = STEPS * K
+    by_cols = pl.BlockSpec((count, cols // turns), lambda n, chip: (0, n))
+    by_rows = pl.BlockSpec((rows // turns, cols), lambda n, chip: (n, 0))
+    return pl.pallas_call(
+        finish_kernel,
+        grid_spec=pltpu.PrefetchScalarGridSpec(
+            num_scalar_prefetch=1,
+            grid=(turns,),
+            in_specs=[
+                by_cols,
+                pl.BlockSpec((count, 2 * rows), lambda n, chip: (0, chip[0])),
+                pl.BlockSpec((2, rows, cols // turns), lambda n, chip: (0, 0, n)),
+                by_rows,
+                by_rows,
+                pl.BlockSpec((LANES, LANES), lambda n, chip: (0, 0)),
+            ],
+            out_specs=(by_cols, by_rows, pl.BlockSpec((size, size), lambda n, chip: (0, 0))),
+        ),
+        out_shape=(
+            jax.ShapeDtypeStruct((count, cols), F32),
+            jax.ShapeDtypeStruct((rows, cols), F32),
+            jax.ShapeDtypeStruct((size, size), F32),
+        ),
+    )(chip, partial, tokens, last, momentum, gradient, krylov)
 
 
 def local(nf, nt, tokens, weight, momentum, gradient, probes):
-    moment = 0.9 * momentum + gradient.astype(F32)
-    summed, krylov = step_call(tokens, weight, probes, moment, nf, nt)
-    size = STEPS * K
-    return (summed, moment, krylov[:size, :size])
+    partial, last, krylov = step_call(tokens, weight, momentum, gradient, probes, nf, nt)
+    chip = lax.div(lax.axis_index("fsdp"), 2)
+    far = 4 * lax.rem(lax.div(chip, 4) + 2, 4) + lax.rem(chip + 2, 4)
+    return finish(far.reshape(1), partial, tokens, last, momentum, gradient, krylov)
 
 
 def solution(mesh):

time: 203 us -> 204 us (level)
  Pallas kernels: 191 us -> 203 us
  local copies, waits for them, and re-layouts: 7.71 us -> 0 us
  other arithmetic: 3.63 us -> 0 us
    pallas_call x0 -> x1, Pallas kernels: none -> 10.8 us  [finish(): pl.pallas_call(finish_kernel, grid_spec=pltpu.PrefetchScalarGridSpec(num_...]
    unnamed x1 -> x0, local copies, waits for them, and re-layouts: 6.28 us -> none
    add x1 -> x0, other arithmetic: 3.63 us -> none  [local(): moment = 0.9 * momentum + gradient.astype(F32)]
where the time goes in v5:
time: 204 us
  Pallas kernels  203 us (100%)
    pallas_call x1, Pallas kernels, step_call(): pl.pallas_call(functools.partial(step_kernel, nf, nt), out_shape=(jax.Sha...  192 us
    pallas_call x1, Pallas kernels, finish(): pl.pallas_call(finish_kernel, grid_spec=pltpu.PrefetchScalarGridSpec(num_...  10.8 us

profile of v5, /device:TPU:1, one launch (start us, length us, event | category | flops | bytes accessed | tf_op | source)
XLA Modules:
  0.0 203.6 jit_solution(12845791289916835420)
XLA Ops:
  0.7 192.1 %shard_map.76 = (f32[768,2048]{1,0:T(8,128)}, bf16[2,256,2048]{2,1,0:T(8,128)(2,1)}, f32[128,128]{1,0:T(8,128)}) custom-call(bf16[768,8192]{1,0:T(8,128)(2,1)} %tokens_ref.3, bf16[256,2048]{1,0:T(8,128)(2,1)} %weight_ref.1, f32[32,2048]{1,0:T(8,128)} %probes_ref.1, f32[256,2048]{1,0:T(8,128)} %momentum_ref.3, bf16[256,2048]{1,0:T(8,128)(2,1)} %gradient_ref.3), custom_call_target="tpu_custom_call" | custom-call | tf_op jit(solution)/shard_map/pallas_call | solution.py:542
  192.8 10.8 %shard_map.77 = (f32[768,2048]{1,0:T(8,128)}, f32[256,2048]{1,0:T(8,128)}, f32[96,96]{1,0:T(8,128)}) custom-call(s32[1]{0:T(128)} %bitcast.chip_ref, f32[768,2048]{1,0:T(8,128)} %get-tuple-element.6.partial_ref, bf16[768,8192]{1,0:T(8,128)(2,1)} %tokens_ref.3, bf16[2,256,2048]{2,1,0:T(8,128)(2,1)} %get-tuple-element.7.last_ref, f32[256,2048]{1,0:T(8,128)} %momentum_ref.3, ...), custom_call_target="tpu_custom_call" | custom-call | tf_op jit(solution)/shard_map/pallas_call | solution.py:620

commit v6 on v5

--- a/solution.py
+++ b/solution.py
@@ -157,33 +157,28 @@
     return tuple(out)
 
 
-EARLY = spans(0, (16, 16, 16, 16))
-LATE = spans(64, (48, 48, 48, 48))
-DURING_TENSOR = ((), (0, 1), (2, 3, 4))
-AFTER = (5, 6, 7)
+BANDS = spans(0, (64, 64, 64, 64))
 
 
 class Flow:
-    def __init__(self, wall, mall, rows, recv, send, sib_recv, sib_send, device_at, sibling):
-        self.wall, self.mall, self.rows = wall, mall, rows
+    def __init__(self, wall, rows, recv, send, sib_recv, sib_send, device_at, sibling):
+        self.wall, self.rows = wall, rows
         self.recv, self.send, self.sib_recv, self.sib_send = recv, send, sib_recv, sib_send
         self.device_at, self.sibling = device_at, sibling
         self.first, self.last = rows[0][0], rows[-1][1]
-        self.kinds = 2 if mall is not None else 1
 
     def copies(self, owner, low, high, send, recv, to):
         band = pl.ds(low, high - low)
-        for ref in (self.wall, self.mall)[: self.kinds]:
-            pltpu.make_async_remote_copy(
-                src_ref=ref.at[owner, band],
-                dst_ref=ref.at[owner, band],
-                send_sem=send,
-                recv_sem=recv,
-                device_id=to,
-            ).start()
+        pltpu.make_async_remote_copy(
+            src_ref=self.wall.at[owner, band],
+            dst_ref=self.wall.at[owner, band],
+            send_sem=send,
+            recv_sem=recv,
+            device_id=to,
+        ).start()
 
     def bytes_of(self, count, high_less_low, sem):
-        ref = self.wall.at[pl.ds(0, count), pl.ds(0, self.kinds * high_less_low)]
+        ref = self.wall.at[pl.ds(0, count), pl.ds(0, high_less_low)]
         return pltpu.make_async_remote_copy(
             src_ref=ref, dst_ref=ref, send_sem=sem, recv_sem=sem, device_id=self.sibling
         )
@@ -224,20 +219,22 @@
     nf,
     nt,
     tokens_ref,
-    weight_ref,
+    weight_hbm,
     probes_ref,
-    momentum_ref,
-    gradient_ref,
+    momentum_hbm,
+    gradient_hbm,
     partial_ref,
     last_ref,
     krylov_ref,
     wall,
-    mall,
     acc,
     toks,
     block,
     basis,
     small,
+    weight_ref,
+    momentum_ref,
+    gradient_ref,
     parts,
     gbuf,
     tbuf,
@@ -245,16 +242,13 @@
     frecv,
     gathered,
     drecv,
-    early_recv,
-    early_send,
-    early_sib_recv,
-    early_sib_send,
     late_recv,
     late_send,
     late_sib_recv,
     late_sib_send,
     tok_sem,
     out_sem,
+    in_sem,
     g_send,
     g_recv,
     t_send,
@@ -291,6 +285,14 @@
     def tensor_at(k):
         return {"tensor": lax.rem(mt + k, nt)}
 
+    loads = [
+        pltpu.make_async_copy(source, target, in_sem.at[at])
+        for at, (source, target) in enumerate(
+            ((momentum_hbm, momentum_ref), (gradient_hbm, gradient_ref), (weight_hbm, weight_ref))
+        )
+    ]
+    for load in loads:
+        load.start()
     barrier = pltpu.get_barrier_semaphore()
 
     @pl.loop(1, nf)
@@ -304,8 +306,7 @@
     lane = lax.broadcasted_iota(jnp.int32, (K, LANES), 1)
 
     def to_all(src, dst, send, recv):
-        @pl.loop(1, nf)
-        def _(k):
+        for k in range(1, nf):
             pltpu.make_async_remote_copy(
                 src_ref=src(lax.rem(mf + k, nf)),
                 dst_ref=dst,
@@ -333,17 +334,10 @@
             device_id=fsdp_at(1),
         )
 
-    early = Flow(wall, mall, EARLY, early_recv, early_send, early_sib_recv, early_sib_send, device_at, sibling)
-    late = Flow(wall, None, LATE, late_recv, late_send, late_sib_recv, late_sib_send, device_at, sibling)
-    ahead = EARLY[-1][1]
+    flow = Flow(wall, BANDS, late_recv, late_send, late_sib_recv, late_sib_send, device_at, sibling)
 
     def owner_at(source):
         return 2 * chip_at(source) + core
-
-    def early_events(*numbers):
-        for number in numbers:
-            for source in GROUPS[number]:
-                early.events(owner_at(source), source)
 
     block[...] = probes_ref[...]
     small[...] = jnp.zeros_like(small)
@@ -356,11 +350,11 @@
         to_tensor(gbuf.at[step, mt], g_send.at[step], g_recv.at[step])
 
     send_gram(0, probes_ref[...])
+    loads[0].wait()
+    loads[1].wait()
     moment = 0.9 * momentum_ref[...] + gradient_ref[...].astype(F32)
     for at, value in enumerate(split(moment)):
         parts[at] = value
-    wall[mf, :ahead] = weight_ref[:ahead]
-    mall[mf] = parts[0, :ahead]
     diags, uppers = [], []
     for step in range(STEPS):
         now = block[...]
@@ -368,8 +362,6 @@
             send_gram(step, now)
         tbuf[step, mt] = split_dot(now, parts, 1)
         to_tensor(tbuf.at[step, mt], t_send.at[step], t_recv.at[step])
-        if step == 0:
-            early.begin(mf)
         all_of(gbuf.at[step], g_send.at[step], g_recv.at[step], nt - 1).wait_recv()
         gram = gbuf[step, 0]
         for other in range(1, nt):
@@ -377,7 +369,6 @@
         upper_next, inverse_low = eliminate(unpack(gram))
         if step:
             uppers.append(upper_next)
-        early_events(*DURING_TENSOR[step])
         all_of(tbuf.at[step], t_send.at[step], t_recv.at[step], nt - 1).wait_recv()
         total = tbuf[step, 0]
         for other in range(1, nt):
@@ -453,13 +444,10 @@
     top = top_value(krylov)
     krylov_ref[...] = krylov / top
     scale = 1.0 / jnp.sqrt(top)
-    fresh = 0.9 * momentum_ref[ahead:] + gradient_ref[ahead:].astype(F32)
-    fresh = weight_ref[ahead:].astype(F32) - fresh * scale
-    wall[mf, ahead:] = fresh.astype(jnp.bfloat16)
-    late.begin(mf)
-
-    early_events(*AFTER)
-    early.sent()
+    loads[2].wait()
+    fresh = 0.9 * momentum_ref[...] + gradient_ref[...].astype(F32)
+    wall[mf] = (weight_ref[...].astype(F32) - fresh * scale).astype(jnp.bfloat16)
+    flow.begin(mf)
 
     order = [(0, 0)] + [source for group in GROUPS for source in group]
 
@@ -471,56 +459,39 @@
 
     tokens_of(0).start()
 
-    def combine(source):
-        owner = 2 * chip_at(source)
-        early.from_sibling(owner + 1 - core, source)
-        for at in range(2):
-
-            @pl.loop(0, ahead // 16)
-            def _(n):
-                band = pl.ds(pl.multiple_of(n * 16, 16), 16)
-                value = wall[owner + at, band].astype(F32)
-                value = value - mall[owner + at, band].astype(F32) * scale
-                wall[owner + at, band] = value.astype(jnp.bfloat16)
-
     def multiply(source):
         number = order.index(source)
         if number + 2 < len(order):
             tokens_of(number + 1).start()
         left_owner = 2 * chip_at(source)
-        combine(source)
-        late.from_sibling(left_owner + 1 - core, source)
+        flow.from_sibling(left_owner + 1 - core, source)
         tokens_of(number).wait()
         left = toks[number % 2]
 
-        @pl.loop(0, cols // 512)
+        @pl.loop(0, cols // 1024)
         def _(n):
-            at = pl.ds(pl.multiple_of(n * 512, 512), 512)
-            right = wall[pl.ds(left_owner, 2), :, at].reshape(2 * rows, 512)
+            at = pl.ds(pl.multiple_of(n * 1024, 1024), 1024)
+            right = wall[pl.ds(left_owner, 2), :, at].reshape(2 * rows, 1024)
             product = jnp.dot(left, right, preferred_element_type=F32)
             if number:
                 acc[:, at] += product
             else:
                 acc[:, at] = product
 
-    before = ((0, 0),)
-    for group in GROUPS[:-1]:
-        for source in group:
-            late.events(owner_at(source), source)
-        for source in before:
-            multiply(source)
-        before = group
-    for source in before:
-        multiply(source)
+    last = order[-1]
+    for number, source in enumerate(order[1:-1]):
+        flow.events(owner_at(source), source)
+        if number != 1:
+            multiply(order[number - (number > 1)])
+    multiply(order[-3])
+    multiply(order[-2])
     partial = pltpu.make_async_copy(acc, partial_ref, out_sem)
     partial.start()
-    last = GROUPS[-1][0]
-    combine(last)
-    late.events(owner_at(last), last)
-    late.from_sibling(2 * chip_at(last) + 1 - core, last)
+    flow.events(owner_at(last), last)
+    flow.from_sibling(2 * chip_at(last) + 1 - core, last)
     final = pltpu.make_async_copy(wall.at[pl.ds(2 * chip_at(last), 2)], last_ref, tok_sem.at[0])
     final.start()
-    late.sent()
+    flow.sent()
     for step in range(STEPS):
         all_of(gbuf.at[step], g_send.at[step], g_recv.at[step], nt - 1).wait_send()
         all_of(tbuf.at[step], t_send.at[step], t_recv.at[step], nt - 1).wait_send()
@@ -546,16 +517,18 @@
             jax.ShapeDtypeStruct((2, rows, cols), jnp.bfloat16),
             jax.ShapeDtypeStruct((LANES, LANES), F32),
         ),
-        in_specs=[anywhere, vmem, vmem, vmem, vmem],
+        in_specs=[anywhere, anywhere, vmem, anywhere, anywhere],
         out_specs=(anywhere, anywhere, vmem),
         scratch_shapes=[
             pltpu.VMEM((nf, rows, cols), jnp.bfloat16),
-            pltpu.VMEM((nf, EARLY[-1][1], cols), jnp.bfloat16),
             pltpu.VMEM((count, cols), F32),
             pltpu.VMEM((2, count, 2 * rows), jnp.bfloat16),
             pltpu.VMEM((K, cols), F32),
             pltpu.VMEM((STEPS - 1, K, cols), F32),
             pltpu.VMEM((K, LANES), F32),
+            pltpu.VMEM((rows, cols), jnp.bfloat16),
+            pltpu.VMEM((rows, cols), F32),
+            pltpu.VMEM((rows, cols), jnp.bfloat16),
             pltpu.VMEM((3, rows, cols), jnp.bfloat16),
             pltpu.VMEM((STEPS, nt, 8, LANES), F32),
             pltpu.VMEM((STEPS, nt, K, rows), F32),
@@ -567,12 +540,9 @@
             dma((4,)),
             dma((16,)),
             dma(()),
-            dma((4, 16)),
-            dma((4,)),
-            dma((16,)),
-            dma(()),
             dma((2,)),
             dma(()),
+            dma((3,)),
             dma((STEPS,)),
             dma((STEPS,)),
             dma((STEPS,)),
@@ -585,7 +555,7 @@
             dma((STEPS,)),
         ],
         compiler_params=pltpu.CompilerParams(
-            collective_id=0, has_side_effects=True, vmem_limit_bytes=63 * 1024 * 1024
+            collective_id=0, has_side_effects=True, vmem_limit_bytes=56 * 1024 * 1024
         ),
     )(tokens, weight, probes, momentum, gradient)
 
@@ -613,7 +583,7 @@
 def finish(chip, partial, tokens, last, momentum, gradient, krylov):
     count, cols = partial.shape
     rows = momentum.shape[0]
-    turns = 8
+    turns = 4
     size = STEPS * K
     by_cols = pl.BlockSpec((count, cols // turns), lambda n, chip: (0, n))
     by_rows = pl.BlockSpec((rows // turns, cols), lambda n, chip: (n, 0))

time: 204 us -> 177 us (0.87)
  Pallas kernels: 203 us -> 176 us
    pallas_call x1, Pallas kernels: 192 us -> 167 us  [step_call(): pl.pallas_call(functools.partial(step_kernel, nf, nt), out_shape=(jax.Sha...]
where the time goes in v6:
time: 177 us
  Pallas kernels  176 us (99%)
    pallas_call x1, Pallas kernels, step_call(): pl.pallas_call(functools.partial(step_kernel, nf, nt), out_shape=(jax.Sha...  167 us
    pallas_call x1, Pallas kernels, finish(): pl.pallas_call(finish_kernel, grid_spec=pltpu.PrefetchScalarGridSpec(num_...  8.92 us

profile of v6, /device:TPU:1, one launch (start us, length us, event | category | flops | bytes accessed | tf_op | source)
XLA Modules:
  0.0 176.9 jit_solution(607754584588125681)
XLA Ops:
  0.7 167.3 %shard_map.76 = (f32[768,2048]{1,0:T(8,128)}, bf16[2,256,2048]{2,1,0:T(8,128)(2,1)}, f32[128,128]{1,0:T(8,128)}) custom-call(bf16[768,8192]{1,0:T(8,128)(2,1)} %tokens_ref.3, bf16[256,2048]{1,0:T(8,128)(2,1)} %weight_hbm.1, f32[32,2048]{1,0:T(8,128)} %probes_ref.1, f32[256,2048]{1,0:T(8,128)} %momentum_ref.1, bf16[256,2048]{1,0:T(8,128)(2,1)} %gradient_ref.1), custom_call_target="tpu_custom_call" | custom-call | tf_op jit(solution)/shard_map/pallas_call | solution.py:513
  168.0 8.9 %shard_map.77 = (f32[768,2048]{1,0:T(8,128)}, f32[256,2048]{1,0:T(8,128)}, f32[96,96]{1,0:T(8,128)}) custom-call(s32[1]{0:T(128)} %bitcast.chip_ref, f32[768,2048]{1,0:T(8,128)} %get-tuple-element.6.partial_ref, bf16[768,8192]{1,0:T(8,128)(2,1)} %tokens_ref.3, bf16[2,256,2048]{2,1,0:T(8,128)(2,1)} %get-tuple-element.7.last_ref, f32[256,2048]{1,0:T(8,128)} %momentum_ref.1, ...), custom_call_target="tpu_custom_call" | custom-call | tf_op jit(solution)/shard_map/pallas_call | solution.py:590

commit v7 on v6

--- a/solution.py
+++ b/solution.py
@@ -160,6 +160,12 @@
 BANDS = spans(0, (64, 64, 64, 64))
 
 
+PARTNERS = sorted(
+    ((i, j, other) for i in (1, 2, -1, 0) for j in (2, 1, -1, 0) for other in (0, 1) if (i, j, other) != (0, 0, 0)),
+    key=lambda at: -(abs(at[0]) + abs(at[1])),
+)
+
+
 class Flow:
     def __init__(self, wall, rows, recv, send, sib_recv, sib_send, device_at, sibling):
         self.wall, self.rows = wall, rows
@@ -205,6 +211,12 @@
             for to in onward(piece, source):
                 self.pass_on(t, owner, source, to)
         self.to_sibling(owner, source)
+
+    def last_event(self, owner, source):
+        for t, (low, high) in enumerate(self.rows):
+            self.bytes_of(1, high - low, self.recv.at[t, slot(source)]).wait_recv()
+            there = self.sib_recv.at[slot((source[1], source[0]))]
+            self.copies(owner, low, high, self.sib_send, there, self.sibling)
 
     def from_sibling(self, owner, source):
         self.bytes_of(1, self.last - self.first, self.sib_recv.at[slot(source)]).wait_recv()
@@ -225,9 +237,9 @@
     gradient_hbm,
     partial_ref,
     last_ref,
+    left_ref,
     krylov_ref,
     wall,
-    acc,
     toks,
     block,
     basis,
@@ -247,8 +259,8 @@
     late_sib_recv,
     late_sib_send,
     tok_sem,
-    out_sem,
     in_sem,
+    left_sem,
     g_send,
     g_recv,
     t_send,
@@ -306,17 +318,18 @@
     lane = lax.broadcasted_iota(jnp.int32, (K, LANES), 1)
 
     def to_all(src, dst, send, recv):
-        for k in range(1, nf):
+        for i, j, other in PARTNERS:
+            to = 2 * chip_at((i, j)) + (1 - core if other else core)
             pltpu.make_async_remote_copy(
-                src_ref=src(lax.rem(mf + k, nf)),
+                src_ref=src(to),
                 dst_ref=dst,
                 send_sem=send,
                 recv_sem=recv,
-                device_id=fsdp_at(k),
+                device_id={"fsdp": to},
             ).start()
 
     def to_tensor(ref, send, recv):
-        for k in range(1, nt):
+        for k in (2, 1, 3):
             pltpu.make_async_remote_copy(
                 src_ref=ref,
                 dst_ref=ref,
@@ -458,6 +471,9 @@
         )
 
     tokens_of(0).start()
+    columns = pl.ds(pl.multiple_of(chip_at(order[-1]) * 2 * rows, 2 * rows), 2 * rows)
+    final = pltpu.make_async_copy(tokens_ref.at[:, columns], left_ref, left_sem)
+    final.start()
 
     def multiply(source):
         number = order.index(source)
@@ -474,9 +490,9 @@
             right = wall[pl.ds(left_owner, 2), :, at].reshape(2 * rows, 1024)
             product = jnp.dot(left, right, preferred_element_type=F32)
             if number:
-                acc[:, at] += product
+                partial_ref[:, at] += product
             else:
-                acc[:, at] = product
+                partial_ref[:, at] = product
 
     last = order[-1]
     for number, source in enumerate(order[1:-1]):
@@ -485,12 +501,10 @@
             multiply(order[number - (number > 1)])
     multiply(order[-3])
     multiply(order[-2])
-    partial = pltpu.make_async_copy(acc, partial_ref, out_sem)
-    partial.start()
-    flow.events(owner_at(last), last)
+    flow.last_event(owner_at(last), last)
     flow.from_sibling(2 * chip_at(last) + 1 - core, last)
-    final = pltpu.make_async_copy(wall.at[pl.ds(2 * chip_at(last), 2)], last_ref, tok_sem.at[0])
-    final.start()
+    last_ref[...] = wall[pl.ds(2 * chip_at(last), 2)]
+    final.wait()
     flow.sent()
     for step in range(STEPS):
         all_of(gbuf.at[step], g_send.at[step], g_recv.at[step], nt - 1).wait_send()
@@ -499,8 +513,6 @@
         if step + 1 < STEPS:
             all_of(fsend.at[step], rs_send.at[step], rs_recv.at[step], nf - 1).wait_send()
             all_of(gathered.at[step], ag_send.at[step], ag_recv.at[step], nf - 1).wait_send()
-    partial.wait()
-    final.wait()
 
 
 def step_call(tokens, weight, momentum, gradient, probes, nf, nt):
@@ -513,15 +525,15 @@
     return pl.pallas_call(
         functools.partial(step_kernel, nf, nt),
         out_shape=(
-            jax.ShapeDtypeStruct((count, cols), F32),
-            jax.ShapeDtypeStruct((2, rows, cols), jnp.bfloat16),
-            jax.ShapeDtypeStruct((LANES, LANES), F32),
+            pltpu.VMEM((count, cols), F32),
+            pltpu.VMEM((2, rows, cols), jnp.bfloat16),
+            pltpu.VMEM((count, 2 * rows), jnp.bfloat16),
+            pltpu.VMEM((LANES, LANES), F32),
         ),
         in_specs=[anywhere, anywhere, vmem, anywhere, anywhere],
-        out_specs=(anywhere, anywhere, vmem),
+        out_specs=(vmem, vmem, vmem, vmem),
         scratch_shapes=[
             pltpu.VMEM((nf, rows, cols), jnp.bfloat16),
-            pltpu.VMEM((count, cols), F32),
             pltpu.VMEM((2, count, 2 * rows), jnp.bfloat16),
             pltpu.VMEM((K, cols), F32),
             pltpu.VMEM((STEPS - 1, K, cols), F32),
@@ -541,8 +553,8 @@
             dma((16,)),
             dma(()),
             dma((2,)),
+            dma((3,)),
             dma(()),
-            dma((3,)),
             dma((STEPS,)),
             dma((STEPS,)),
             dma((STEPS,)),
@@ -555,15 +567,14 @@
             dma((STEPS,)),
         ],
         compiler_params=pltpu.CompilerParams(
-            collective_id=0, has_side_effects=True, vmem_limit_bytes=56 * 1024 * 1024
+            collective_id=0, has_side_effects=True, vmem_limit_bytes=48 * 1024 * 1024
         ),
     )(tokens, weight, probes, momentum, gradient)
 
 
 def finish_kernel(
-    chip_ref,
     partial_ref,
-    tokens_ref,
+    left_ref,
     last_ref,
     momentum_ref,
     gradient_ref,
@@ -573,48 +584,43 @@
     scaled_ref,
 ):
     both, rows, cols = last_ref.shape
-    right = last_ref[...].reshape(both * rows, cols)
-    out_ref[...] = partial_ref[...] + jnp.dot(tokens_ref[...], right, preferred_element_type=F32)
+    width = out_ref.shape[1]
+    at = pl.ds(pl.multiple_of(pl.program_id(0) * width, width), width)
+    right = last_ref[:, :, at].reshape(both * rows, width)
+    out_ref[...] = partial_ref[:, at] + jnp.dot(left_ref[...], right, preferred_element_type=F32)
     moment_ref[...] = 0.9 * momentum_ref[...] + gradient_ref[...].astype(F32)
     size = scaled_ref.shape[0]
     scaled_ref[...] = krylov_ref[:size, :size]
 
 
-def finish(chip, partial, tokens, last, momentum, gradient, krylov):
+def finish(partial, left, last, momentum, gradient, krylov):
     count, cols = partial.shape
     rows = momentum.shape[0]
     turns = 4
     size = STEPS * K
-    by_cols = pl.BlockSpec((count, cols // turns), lambda n, chip: (0, n))
-    by_rows = pl.BlockSpec((rows // turns, cols), lambda n, chip: (n, 0))
+    vmem = pl.BlockSpec(memory_space=pltpu.VMEM)
+    by_cols = pl.BlockSpec((count, cols // turns), lambda n: (0, n))
+    by_rows = pl.BlockSpec((rows // turns, cols), lambda n: (n, 0))
     return pl.pallas_call(
         finish_kernel,
-        grid_spec=pltpu.PrefetchScalarGridSpec(
-            num_scalar_prefetch=1,
-            grid=(turns,),
-            in_specs=[
-                by_cols,
-                pl.BlockSpec((count, 2 * rows), lambda n, chip: (0, chip[0])),
-                pl.BlockSpec((2, rows, cols // turns), lambda n, chip: (0, 0, n)),
-                by_rows,
-                by_rows,
-                pl.BlockSpec((LANES, LANES), lambda n, chip: (0, 0)),
-            ],
-            out_specs=(by_cols, by_rows, pl.BlockSpec((size, size), lambda n, chip: (0, 0))),
-        ),
+        grid=(turns,),
+        in_specs=[vmem, vmem, vmem, by_rows, by_rows, vmem],
+        out_specs=(by_cols, by_rows, pl.BlockSpec((size, size), lambda n: (0, 0))),
         out_shape=(
             jax.ShapeDtypeStruct((count, cols), F32),
             jax.ShapeDtypeStruct((rows, cols), F32),
             jax.ShapeDtypeStruct((size, size), F32),
         ),
-    )(chip, partial, tokens, last, momentum, gradient, krylov)
+        compiler_params=pltpu.CompilerParams(vmem_limit_bytes=24 * 1024 * 1024),
+    )(partial, left, last, momentum, gradient, krylov)
 
 
 def local(nf, nt, tokens, weight, momentum, gradient, probes):
-    partial, last, krylov = step_call(tokens, weight, momentum, gradient, probes, nf, nt)
-    chip = lax.div(lax.axis_index("fsdp"), 2)
-    far = 4 * lax.rem(lax.div(chip, 4) + 2, 4) + lax.rem(chip + 2, 4)
-    return finish(far.reshape(1), partial, tokens, last, momentum, gradient, krylov)
+    held = step_call(tokens, weight, momentum, gradient, probes, nf, nt)
+    partial, last, left, krylov = (
+        pltpu.with_memory_space_constraint(value, pltpu.VMEM) for value in held
+    )
+    return finish(partial, left, last, momentum, gradient, krylov)
 
 
 def solution(mesh):

time: 177 us -> 168 us (0.949)
  Pallas kernels: 176 us -> 167 us
    pallas_call x2, Pallas kernels: 176 us -> 167 us  [the longest x1 163 us: step_call(): pl.pallas_call(functools.partial(step_kernel, nf, nt), out_shape=(pltpu.V...]
where the time goes in v7:
time: 168 us
  Pallas kernels  167 us (99%)
    pallas_call x1, Pallas kernels, step_call(): pl.pallas_call(functools.partial(step_kernel, nf, nt), out_shape=(pltpu.V...  163 us
    pallas_call x1, Pallas kernels, finish(): pl.pallas_call(finish_kernel, grid=(turns,), in_specs=[vmem, vmem, vmem,...  4.51 us

profile of v7, /device:TPU:1, one launch (start us, length us, event | category | flops | bytes accessed | tf_op | source)
XLA Modules:
  0.0 168.1 jit_solution(510988306164597830)
XLA Ops:
  0.6 0.0 copy-start.1
  0.6 0.0 copy-start
  0.7 162.9 %shard_map.76 = (f32[768,2048]{1,0:T(8,128)S(1)}, bf16[2,256,2048]{2,1,0:T(8,128)(2,1)S(1)}, bf16[768,512]{1,0:T(8,128)(2,1)S(1)}, f32[128,128]{1,0:T(8,128)S(1)}) custom-call(bf16[768,8192]{1,0:T(8,128)(2,1)} %tokens_ref.1, bf16[256,2048]{1,0:T(8,128)(2,1)} %weight_hbm.1, f32[32,2048]{1,0:T(8,128)} %probes_ref.1, f32[256,2048]{1,0:T(8,128)} %momentum_ref.1, ...), custom_call_target="tpu_custom_call" | custom-call | tf_op jit(solution)/shard_map/pallas_call | solution.py:525
  163.6 0.0 copy-done.1
  163.6 0.0 copy-done
  163.6 4.5 %shard_map.77 = (f32[768,2048]{1,0:T(8,128)}, f32[256,2048]{1,0:T(8,128)}, f32[96,96]{1,0:T(8,128)}) custom-call(f32[768,2048]{1,0:T(8,128)S(1)} %get-tuple-element.7.partial_ref, bf16[768,512]{1,0:T(8,128)(2,1)S(1)} %get-tuple-element.8.left_ref, bf16[2,256,2048]{2,1,0:T(8,128)(2,1)S(1)} %get-tuple-element.9.last_ref, f32[256,2048]{1,0:T(8,128)S(1)} %copy-done, ...), custom_call_target="tpu_custom_call" | custom-call | tf_op jit(solution)/shard_map/pallas_call | solution.py:604
Async XLA Ops:
  0.6 163.0 %copy-start.1 = (bf16[256,2048]{1,0:T(8,128)(2,1)S(1)}, bf16[256,2048]{1,0:T(8,128)(2,1)}, u32[]{:S(2)}) copy-start(bf16[256,2048]{1,0:T(8,128)(2,1)} %gradient_ref.1) | copy-start | bytes 3145732
  0.6 163.0 %copy-start = (f32[256,2048]{1,0:T(8,128)S(1)}, f32[256,2048]{1,0:T(8,128)}, u32[]{:S(2)}) copy-start(f32[256,2048]{1,0:T(8,128)} %momentum_ref.1) | copy-start | bytes 6291460

commit v8 on v7

--- a/solution.py
+++ b/solution.py
@@ -113,15 +113,10 @@
 
 
 PIECES = (("a", 1), ("a", -1), ("b", 1), ("b", -1))
-GROUPS = (
-    ((1, 0), (0, 1)),
-    ((-1, 0), (0, -1)),
-    ((1, 1), (-1, -1)),
-    ((1, -1), (-1, 1)),
-    ((2, 0), (0, 2)),
-    ((2, 1), (1, 2)),
-    ((2, -1), (-1, 2)),
-    ((2, 2),),
+LAST = (2, 2)
+ORDER = (
+    (0, 0), (1, 0), (0, 1), (-1, 0), (0, -1), (1, 1), (-1, -1), (1, -1), (-1, 1),
+    (2, 0), (0, 2), (2, 1), (1, 2), (2, -1), (-1, 2), LAST,
 )
 
 
@@ -144,6 +139,30 @@
     return out
 
 
+def level(*places):
+    out = []
+    for u, v in places:
+        for t, (first, sign) in enumerate(PIECES):
+            at = (-u * sign, -v * sign)
+            at = at if first == "a" else at[::-1]
+            out.append((t, (signed(at[0]), signed(at[1]))))
+    return out
+
+
+PLAN = (
+    (level((1, 0), (-1, 0)), ((0, 0),)),
+    (level((0, 1), (0, -1)), ()),
+    (level((2, 0)), ((1, 0),)),
+    (level((1, 1), (-1, 1)), ((0, 1),)),
+    (level((1, -1), (-1, -1)), ((-1, 0),)),
+    (level((2, 1)), ((0, -1),)),
+    (level((0, 2)), ((1, 1),)),
+    (level((1, 2)), ((-1, -1), (1, -1))),
+    (level((-1, 2)), ((-1, 1), (2, 0))),
+    (level((2, -1)), ((0, 2), (2, 1), (1, 2), (2, -1), (-1, 2))),
+)
+
+
 def slot(at):
     i, j = mod4(at)
     return 4 * i + j
@@ -198,19 +217,15 @@
         there = self.sib_recv.at[slot((source[1], source[0]))]
         self.copies(owner, self.first, self.last, self.sib_send, there, self.sibling)
 
-    def begin(self, owner):
-        for rank in range(4):
-            for t, piece in enumerate(PIECES):
-                self.pass_on(t, owner, (0, 0), onward(piece, (0, 0))[rank])
-        self.to_sibling(owner, (0, 0))
-
-    def events(self, owner, source):
-        for t, piece in enumerate(PIECES):
-            low, high = self.rows[t]
-            self.bytes_of(1, high - low, self.recv.at[t, slot(source)]).wait_recv()
-            for to in onward(piece, source):
-                self.pass_on(t, owner, source, to)
-        self.to_sibling(owner, source)
+    def begin(self, t, owner):
+        for to in onward(PIECES[t], (0, 0)):
+            self.pass_on(t, owner, (0, 0), to)
+
+    def event(self, t, owner, source):
+        low, high = self.rows[t]
+        self.bytes_of(1, high - low, self.recv.at[t, slot(source)]).wait_recv()
+        for to in onward(PIECES[t], source):
+            self.pass_on(t, owner, source, to)
 
     def last_event(self, owner, source):
         for t, (low, high) in enumerate(self.rows):
@@ -362,12 +377,12 @@
             pl.semaphore_wait(barrier, nf + nt - 2)
         to_tensor(gbuf.at[step, mt], g_send.at[step], g_recv.at[step])
 
-    send_gram(0, probes_ref[...])
     loads[0].wait()
     loads[1].wait()
     moment = 0.9 * momentum_ref[...] + gradient_ref[...].astype(F32)
     for at, value in enumerate(split(moment)):
         parts[at] = value
+    send_gram(0, probes_ref[...])
     diags, uppers = [], []
     for step in range(STEPS):
         now = block[...]
@@ -434,35 +449,36 @@
             to_all(
                 lambda dest: drecv.at[step, mf], drecv.at[step, mf], d_send.at[step], d_recv.at[step]
             )
+            row = lax.broadcasted_iota(jnp.int32, (K, K), 0)
+            eye = jnp.where(row == lax.broadcasted_iota(jnp.int32, (K, K), 1), 1.0, 0.0)
+            lows = []
+            for at in range(STEPS - 1):
+                small[:, :K] = hdot_t(eye, uppers[at][:, :K])
+                lows.append(small[...])
+            bands = [
+                diags[0] + pltpu.roll(lows[0], K, 1),
+                uppers[0] + pltpu.roll(diags[1], K, 1) + pltpu.roll(lows[1], 2 * K, 1),
+                pltpu.roll(uppers[1], K, 1),
+                jnp.zeros((K, LANES), F32),
+            ]
             all_of(drecv.at[step], d_send.at[step], d_recv.at[step], nf - 1).wait_recv()
             diag = unpack(jnp.sum(drecv[step], axis=0))
+            bands[2] = bands[2] + pltpu.roll(diag, 2 * K, 1)
         diags.append(diag)
 
-    eye = jnp.where(lax.broadcasted_iota(jnp.int32, (K, K), 0) == lax.broadcasted_iota(jnp.int32, (K, K), 1), 1.0, 0.0)
-    lows = []
-    for at in range(STEPS - 1):
-        small[:, :K] = hdot_t(eye, uppers[at][:, :K])
-        lows.append(small[...])
-    bands = []
-    for at in range(STEPS):
-        band = pltpu.roll(diags[at], K * at, 1) if at else diags[at]
-        if at + 1 < STEPS:
-            band = band + pltpu.roll(lows[at], K * (at + 1), 1)
-        if at:
-            before = uppers[at - 1]
-            band = band + (pltpu.roll(before, K * (at - 1), 1) if at > 1 else before)
-        bands.append(band)
-    bands.append(jnp.zeros((K, LANES), F32))
     krylov = jnp.concatenate(bands, axis=0)
     top = top_value(krylov)
     krylov_ref[...] = krylov / top
     scale = 1.0 / jnp.sqrt(top)
     loads[2].wait()
-    fresh = 0.9 * momentum_ref[...] + gradient_ref[...].astype(F32)
-    wall[mf] = (weight_ref[...].astype(F32) - fresh * scale).astype(jnp.bfloat16)
-    flow.begin(mf)
-
-    order = [(0, 0)] + [source for group in GROUPS for source in group]
+    for t, (low, high) in enumerate(BANDS):
+        fresh = 0.9 * momentum_ref[low:high] + gradient_ref[low:high].astype(F32)
+        fresh = weight_ref[low:high].astype(F32) - fresh * scale
+        wall[mf, low:high] = fresh.astype(jnp.bfloat16)
+        flow.begin(t, mf)
+    flow.to_sibling(mf, (0, 0))
+
+    order = list(ORDER)
 
     def tokens_of(number):
         columns = pl.ds(pl.multiple_of(chip_at(order[number]) * 2 * rows, 2 * rows), 2 * rows)
@@ -494,13 +510,16 @@
             else:
                 partial_ref[:, at] = product
 
-    last = order[-1]
-    for number, source in enumerate(order[1:-1]):
-        flow.events(owner_at(source), source)
-        if number != 1:
-            multiply(order[number - (number > 1)])
-    multiply(order[-3])
-    multiply(order[-2])
+    seen = {}
+    for events, ready in PLAN:
+        for t, source in events:
+            flow.event(t, owner_at(source), source)
+            seen[source] = seen.get(source, 0) + 1
+            if seen[source] == len(PIECES):
+                flow.to_sibling(owner_at(source), source)
+        for source in ready:
+            multiply(source)
+    last = LAST
     flow.last_event(owner_at(last), last)
     flow.from_sibling(2 * chip_at(last) + 1 - core, last)
     last_ref[...] = wall[pl.ds(2 * chip_at(last), 2)]

time: 168 us -> 174 us (1.036)
  Pallas kernels: 167 us -> 174 us
    pallas_call x1, Pallas kernels: 163 us -> 169 us  [step_call(): pl.pallas_call(functools.partial(step_kernel, nf, nt), out_shape=(pltpu.V...]
where the time goes in v8:
time: 174 us
  Pallas kernels  174 us (100%)
    pallas_call x1, Pallas kernels, step_call(): pl.pallas_call(functools.partial(step_kernel, nf, nt), out_shape=(pltpu.V...  169 us
    pallas_call x1, Pallas kernels, finish(): pl.pallas_call(finish_kernel, grid=(turns,), in_specs=[vmem, vmem, vmem,...  4.5 us

profile of v8, /device:TPU:1, one launch (start us, length us, event | category | flops | bytes accessed | tf_op | source)
XLA Modules:
  0.0 174.3 jit_solution(1618926073468271797)
XLA Ops:
  0.6 0.0 copy-start.1
  0.6 0.0 copy-start
  0.7 169.1 %shard_map.76 = (f32[768,2048]{1,0:T(8,128)S(1)}, bf16[2,256,2048]{2,1,0:T(8,128)(2,1)S(1)}, bf16[768,512]{1,0:T(8,128)(2,1)S(1)}, f32[128,128]{1,0:T(8,128)S(1)}) custom-call(bf16[768,8192]{1,0:T(8,128)(2,1)} %tokens_ref.1, bf16[256,2048]{1,0:T(8,128)(2,1)} %weight_hbm.1, f32[32,2048]{1,0:T(8,128)} %probes_ref.1, f32[256,2048]{1,0:T(8,128)} %momentum_ref.1, ...), custom_call_target="tpu_custom_call" | custom-call | tf_op jit(solution)/shard_map/pallas_call | solution.py:544
  169.8 0.0 copy-done.1
  169.8 0.0 copy-done
  169.8 4.5 %shard_map.77 = (f32[768,2048]{1,0:T(8,128)}, f32[256,2048]{1,0:T(8,128)}, f32[96,96]{1,0:T(8,128)}) custom-call(f32[768,2048]{1,0:T(8,128)S(1)} %get-tuple-element.7.partial_ref, bf16[768,512]{1,0:T(8,128)(2,1)S(1)} %get-tuple-element.8.left_ref, bf16[2,256,2048]{2,1,0:T(8,128)(2,1)S(1)} %get-tuple-element.9.last_ref, f32[256,2048]{1,0:T(8,128)S(1)} %copy-done, ...), custom_call_target="tpu_custom_call" | custom-call | tf_op jit(solution)/shard_map/pallas_call | solution.py:623
Async XLA Ops:
  0.6 169.2 %copy-start.1 = (bf16[256,2048]{1,0:T(8,128)(2,1)S(1)}, bf16[256,2048]{1,0:T(8,128)(2,1)}, u32[]{:S(2)}) copy-start(bf16[256,2048]{1,0:T(8,128)(2,1)} %gradient_ref.1) | copy-start | bytes 3145732
  0.6 169.2 %copy-start = (f32[256,2048]{1,0:T(8,128)S(1)}, f32[256,2048]{1,0:T(8,128)}, u32[]{:S(2)}) copy-start(f32[256,2048]{1,0:T(8,128)} %momentum_ref.1) | copy-start | bytes 6291460

commit v9 on v7

--- a/solution.py
+++ b/solution.py
@@ -373,8 +373,10 @@
         now = block[...]
         if step:
             send_gram(step, now)
-        tbuf[step, mt] = split_dot(now, parts, 1)
-        to_tensor(tbuf.at[step, mt], t_send.at[step], t_recv.at[step])
+        for half in range(2):
+            band = slice(LANES * half, LANES * (half + 1))
+            tbuf[step, mt, half] = split_dot(now, [parts[at, band] for at in range(3)], 1)
+            to_tensor(tbuf.at[step, mt, half], t_send.at[step], t_recv.at[step])
         all_of(gbuf.at[step], g_send.at[step], g_recv.at[step], nt - 1).wait_recv()
         gram = gbuf[step, 0]
         for other in range(1, nt):
@@ -386,6 +388,7 @@
         total = tbuf[step, 0]
         for other in range(1, nt):
             total = total + tbuf[step, other]
+        total = jnp.concatenate([total[0], total[1]], axis=1)
         inverse_low = inverse_low[:, :K]
         reduced = hdot(inverse_low, total)
         small[:, :K] = hdot_t(reduced, reduced)
@@ -434,25 +437,23 @@
             to_all(
                 lambda dest: drecv.at[step, mf], drecv.at[step, mf], d_send.at[step], d_recv.at[step]
             )
+            row = lax.broadcasted_iota(jnp.int32, (K, K), 0)
+            eye = jnp.where(row == lax.broadcasted_iota(jnp.int32, (K, K), 1), 1.0, 0.0)
+            lows = []
+            for at in range(STEPS - 1):
+                small[:, :K] = hdot_t(eye, uppers[at][:, :K])
+                lows.append(small[...])
+            bands = [
+                diags[0] + pltpu.roll(lows[0], K, 1),
+                uppers[0] + pltpu.roll(diags[1], K, 1) + pltpu.roll(lows[1], 2 * K, 1),
+                pltpu.roll(uppers[1], K, 1),
+                jnp.zeros((K, LANES), F32),
+            ]
             all_of(drecv.at[step], d_send.at[step], d_recv.at[step], nf - 1).wait_recv()
             diag = unpack(jnp.sum(drecv[step], axis=0))
+            bands[2] = bands[2] + pltpu.roll(diag, 2 * K, 1)
         diags.append(diag)
 
-    eye = jnp.where(lax.broadcasted_iota(jnp.int32, (K, K), 0) == lax.broadcasted_iota(jnp.int32, (K, K), 1), 1.0, 0.0)
-    lows = []
-    for at in range(STEPS - 1):
-        small[:, :K] = hdot_t(eye, uppers[at][:, :K])
-        lows.append(small[...])
-    bands = []
-    for at in range(STEPS):
-        band = pltpu.roll(diags[at], K * at, 1) if at else diags[at]
-        if at + 1 < STEPS:
-            band = band + pltpu.roll(lows[at], K * (at + 1), 1)
-        if at:
-            before = uppers[at - 1]
-            band = band + (pltpu.roll(before, K * (at - 1), 1) if at > 1 else before)
-        bands.append(band)
-    bands.append(jnp.zeros((K, LANES), F32))
     krylov = jnp.concatenate(bands, axis=0)
     top = top_value(krylov)
     krylov_ref[...] = krylov / top
@@ -543,7 +544,7 @@
             pltpu.VMEM((rows, cols), jnp.bfloat16),
             pltpu.VMEM((3, rows, cols), jnp.bfloat16),
             pltpu.VMEM((STEPS, nt, 8, LANES), F32),
-            pltpu.VMEM((STEPS, nt, K, rows), F32),
+            pltpu.VMEM((STEPS, nt, 2, K, LANES), F32),
             pltpu.VMEM((STEPS - 1, nf, 8, width), F32),
             pltpu.VMEM((STEPS - 1, nf, 8, width), F32),
             pltpu.VMEM((STEPS - 1, nf, 8, width), F32),

time: 168 us -> 167 us (level)
  no operation moved by 1% of the time
where the time goes in v9:
time: 167 us
  Pallas kernels  166 us (99%)
    pallas_call x1, Pallas kernels, step_call(): pl.pallas_call(functools.partial(step_kernel, nf, nt), out_shape=(pltpu.V...  161 us
    pallas_call x1, Pallas kernels, finish(): pl.pallas_call(finish_kernel, grid=(turns,), in_specs=[vmem, vmem, vmem,...  4.51 us

profile of v9, /device:TPU:1, one launch (start us, length us, event | category | flops | bytes accessed | tf_op | source)
XLA Modules:
  0.0 166.7 jit_solution(11410505480750032940)
XLA Ops:
  0.6 0.0 copy-start.1
  0.6 0.0 copy-start
  0.7 161.5 %shard_map.76 = (f32[768,2048]{1,0:T(8,128)S(1)}, bf16[2,256,2048]{2,1,0:T(8,128)(2,1)S(1)}, bf16[768,512]{1,0:T(8,128)(2,1)S(1)}, f32[128,128]{1,0:T(8,128)S(1)}) custom-call(bf16[768,8192]{1,0:T(8,128)(2,1)} %tokens_ref.1, bf16[256,2048]{1,0:T(8,128)(2,1)} %weight_hbm.1, f32[32,2048]{1,0:T(8,128)} %probes_ref.1, f32[256,2048]{1,0:T(8,128)} %momentum_ref.1, ...), custom_call_target="tpu_custom_call" | custom-call | tf_op jit(solution)/shard_map/pallas_call | solution.py:526
  162.2 0.0 copy-done.1
  162.2 0.0 copy-done
  162.2 4.5 %shard_map.77 = (f32[768,2048]{1,0:T(8,128)}, f32[256,2048]{1,0:T(8,128)}, f32[96,96]{1,0:T(8,128)}) custom-call(f32[768,2048]{1,0:T(8,128)S(1)} %get-tuple-element.7.partial_ref, bf16[768,512]{1,0:T(8,128)(2,1)S(1)} %get-tuple-element.8.left_ref, bf16[2,256,2048]{2,1,0:T(8,128)(2,1)S(1)} %get-tuple-element.9.last_ref, f32[256,2048]{1,0:T(8,128)S(1)} %copy-done, ...), custom_call_target="tpu_custom_call" | custom-call | tf_op jit(solution)/shard_map/pallas_call | solution.py:605
Async XLA Ops:
  0.6 161.5 %copy-start.1 = (bf16[256,2048]{1,0:T(8,128)(2,1)S(1)}, bf16[256,2048]{1,0:T(8,128)(2,1)}, u32[]{:S(2)}) copy-start(bf16[256,2048]{1,0:T(8,128)(2,1)} %gradient_ref.1) | copy-start | bytes 3145732
  0.6 161.5 %copy-start = (f32[256,2048]{1,0:T(8,128)S(1)}, f32[256,2048]{1,0:T(8,128)}, u32[]{:S(2)}) copy-start(f32[256,2048]{1,0:T(8,128)} %momentum_ref.1) | copy-start | bytes 6291460
